TPU v7x, 32 devices: a whole 2x2x4 slice. The times are simulated.
32 devices in a mesh: dp: 4 (over y, x), sp: 8 (over z, core).
Axes of the slice: x: 2, y: 2, z: 4, core: 2. Of those that a mesh axis runs over, the one named last changes fastest.
Arguments:
- tokens: bfloat16 [2, 4, 1024, 768], P(None, 'dp', 'sp'), may hold values from -6 to 6
- doc_ids: int32 [2, 4, 1024], P(None, 'dp', 'sp'), may hold values from 0 to 7, as said below
- cotangent: bfloat16 [2, 4, 1024, 768], P(None, 'dp', 'sp'), may hold values from -6 to 6
- query_weight: bfloat16 [768, 768], P(('dp', 'sp')), may hold values from -0.21875 to 0.21875
- key_weight: bfloat16 [768, 768], P(('dp', 'sp')), may hold values from -0.21875 to 0.21875
- value_weight: bfloat16 [768, 768], P(('dp', 'sp')), may hold values from -0.21875 to 0.21875
- output_weight: bfloat16 [768, 768], P(('dp', 'sp')), may hold values from -1.25 to 1.25
- query_bias: bfloat16 [768], P(('dp', 'sp')), may hold values from -1.1953125 to 1.1953125
- value_bias: bfloat16 [768], P(('dp', 'sp')), may hold values from -1.796875 to 1.796875
- output_bias: bfloat16 [768], P(('dp', 'sp')), may hold values from -1.796875 to 1.796875
- first_gain: bfloat16 [768], P(('dp', 'sp')), may hold values from 0.5 to 1.5
- first_shift: bfloat16 [768], P(('dp', 'sp')), may hold values from -1.1953125 to 1.1953125
- inner_weight: bfloat16 [768, 3072], P(('dp', 'sp')), may hold values from -0.21875 to 0.21875
- inner_bias: bfloat16 [3072], P(('dp', 'sp')), may hold values from -1.796875 to 1.796875
- outer_weight: bfloat16 [3072, 768], P(('dp', 'sp')), may hold values from -0.21875 to 0.21875
- outer_bias: bfloat16 [768], P(('dp', 'sp')), may hold values from -1.796875 to 1.796875
- second_gain: bfloat16 [768], P(('dp', 'sp')), may hold values from 0.5 to 1.5
- second_shift: bfloat16 [768], P(('dp', 'sp')), may hold values from -1.1953125 to 1.1953125
Outputs:
- outputs: bfloat16 [2, 4, 1024, 768], P(None, 'dp', 'sp')
- tokens_grad: float32 [2, 4, 1024, 768], P(None, 'dp', 'sp')
- query_weight_grad: float32 [768, 768], P(('dp', 'sp'))
- key_weight_grad: float32 [768, 768], P(('dp', 'sp'))
- value_weight_grad: float32 [768, 768], P(('dp', 'sp'))
- output_weight_grad: float32 [768, 768], P(('dp', 'sp'))
- query_bias_grad: float32 [768], P(('dp', 'sp'))
- value_bias_grad: float32 [768], P(('dp', 'sp'))
- output_bias_grad: float32 [768], P(('dp', 'sp'))
- first_gain_grad: float32 [768], P(('dp', 'sp'))
- first_shift_grad: float32 [768], P(('dp', 'sp'))
- inner_weight_grad: float32 [768, 3072], P(('dp', 'sp'))
- inner_bias_grad: float32 [3072], P(('dp', 'sp'))
- outer_weight_grad: float32 [3072, 768], P(('dp', 'sp'))
- outer_bias_grad: float32 [768], P(('dp', 'sp'))
- second_gain_grad: float32 [768], P(('dp', 'sp'))
- second_shift_grad: float32 [768], P(('dp', 'sp'))
Inputs may be any that keep to these rules, and one draw needn't show every extreme that they name: `doc_ids`: along each of the 2 x 4 sequences the ids never fall; each sequence begins with id 0 and ends with id 7. For each of the 4 sequence positions of a micro-batch, one of the 2 micro-batches holds a document that begins among the first 128 tokens and ends among the last 128.
All inputs are finite; a program needn't handle non-finite values.
Results may differ from a plain program's by a relative error of at most 0.02.
Values may be sent and summed in bfloat16 or wider, within the bound.
No kernel may reach another device: no remote copies, remote signals or barrier semaphores. Data moves between devices by JAX's collectives and lax.ppermute only.
A program may use at most 384 MiB of HBM per device.

v0:
```python
import jax
import jax.numpy as jnp
from jax import lax
from jax.sharding import PartitionSpec as P

HEADS = 12
HEAD = 64


EPS = 1e-12
NEG = -1e30


def product(left_matrix, right_matrix):
    return jnp.dot(left_matrix, right_matrix, preferred_element_type=jnp.float32)


def left_product(left_matrix, right_matrix):
    return lax.dot_general(
        left_matrix, right_matrix, (((0,), (0,)), ((), ())), preferred_element_type=jnp.float32
    )


def right_product(left_matrix, right_matrix):
    return lax.dot_general(
        left_matrix, right_matrix, (((1,), (1,)), ((), ())), preferred_element_type=jnp.float32
    )


def by_heads(matrix):
    return matrix.reshape(matrix.shape[0], HEADS, HEAD)


def norm_forward(summed, gain, shift):
    center = summed - jnp.mean(summed, -1, keepdims=True)
    inverse = lax.rsqrt(jnp.mean(center * center, -1, keepdims=True) + EPS)
    normed = center * inverse
    return (normed * gain + shift, normed, inverse)


def norm_backward(gradient, normed, inverse, gain):
    scaled = gradient * gain
    plain_mean = jnp.mean(scaled, -1, keepdims=True)
    cross_mean = jnp.mean(scaled * normed, -1, keepdims=True)
    return (
        (scaled - plain_mean - normed * cross_mean) * inverse,
        jnp.sum(gradient * normed, 0),
        jnp.sum(gradient, 0),
    )


def attend_forward(queries, key_rows, value_rows, seg_local, seg_all):
    row_count = queries.shape[0]
    scaling = HEAD ** (-0.5)
    query_heads = by_heads(queries)
    key_piece = lax.all_gather(key_rows, "sp", axis=0, tiled=True)
    value_piece = lax.all_gather(value_rows, "sp", axis=0, tiled=True)
    row_peak = jnp.full((HEADS, row_count), NEG, jnp.float32)
    same_doc = (seg_local[:, None] == seg_all[None, :])[None]
    scores = (
        jnp.einsum(
            "qhd,khd->hqk", query_heads, by_heads(key_piece), preferred_element_type=jnp.float32
        )
        * scaling
    )
    scores = jnp.where(same_doc, scores, NEG)
    new_peak = jnp.maximum(row_peak, jnp.max(scores, -1))
    weights = jnp.where(same_doc, jnp.exp(scores - new_peak[..., None]), 0.0)
    row_total = jnp.sum(weights, -1)
    summed = jnp.einsum(
        "hqk,khd->hqd",
        weights.astype(jnp.bfloat16),
        by_heads(value_piece),
        preferred_element_type=jnp.float32,
    )
    return (new_peak, row_total, summed)


def keys_backward(
    queries, key_rows, value_rows, context_grad, log_total, row_delta, seg_local, seg_all
):
    row_count, width = queries.shape
    scaling = HEAD ** (-0.5)
    query_heads = by_heads(queries)
    grad_heads = by_heads(context_grad)
    key_piece = lax.all_gather(key_rows, "sp", axis=0, tiled=True)
    value_piece = lax.all_gather(value_rows, "sp", axis=0, tiled=True)
    piece_rows = key_piece.shape[0]
    key_heads = by_heads(key_piece)
    same_doc = (seg_local[:, None] == seg_all[None, :])[None]
    scores = (
        jnp.einsum("qhd,khd->hqk", query_heads, key_heads, preferred_element_type=jnp.float32)
        * scaling
    )
    weights = jnp.where(same_doc, jnp.exp(scores - log_total[..., None]), 0.0)
    prob_grad = jnp.einsum(
        "qhd,khd->hqk", grad_heads, by_heads(value_piece), preferred_element_type=jnp.float32
    )
    score_grad = (weights * (prob_grad - row_delta[..., None])).astype(jnp.bfloat16)
    query_sum = jnp.einsum(
        "hqk,khd->hqd", score_grad, key_heads, preferred_element_type=jnp.float32
    )
    key_term = jnp.einsum(
        "hqk,qhd->khd", score_grad, query_heads, preferred_element_type=jnp.float32
    ).reshape(piece_rows, width)
    value_term = jnp.einsum(
        "hqk,qhd->khd", weights.astype(jnp.bfloat16), grad_heads, preferred_element_type=jnp.float32
    ).reshape(piece_rows, width)
    pair_sum = jnp.concatenate([key_term, value_term], 1)
    query_sum, pair_sum = (query_sum, pair_sum)
    pair_mine = lax.psum_scatter(pair_sum, "sp", scatter_dimension=0, tiled=True)
    query_sum = jnp.transpose(query_sum, (1, 0, 2)).reshape(row_count, width)
    return (query_sum, pair_mine[:, :width], pair_mine[:, width:])


def body(
    tokens,
    doc_ids,
    cotangent,
    query_weight,
    key_weight,
    value_weight,
    output_weight,
    query_bias,
    value_bias,
    output_bias,
    first_gain,
    first_shift,
    inner_weight,
    inner_bias,
    outer_weight,
    outer_bias,
    second_gain,
    second_shift,
):
    shards = (
        query_weight,
        key_weight,
        value_weight,
        output_weight,
        query_bias,
        value_bias,
        output_bias,
        first_gain,
        first_shift,
        inner_weight,
        inner_bias,
        outer_weight,
        outer_bias,
        second_gain,
        second_shift,
    )
    scaling = HEAD ** (-0.5)
    results = []
    input_grads = []
    totals = ()
    for micro in range(tokens.shape[0]):
        loaded = (
            lax.all_gather(shards[0], ("dp", "sp"), axis=0, tiled=True),
            lax.all_gather(shards[1], ("dp", "sp"), axis=0, tiled=True),
            lax.all_gather(shards[2], ("dp", "sp"), axis=0, tiled=True),
            lax.all_gather(shards[3], ("dp", "sp"), axis=0, tiled=True),
            lax.all_gather(shards[4], ("dp", "sp"), axis=0, tiled=True),
            lax.all_gather(shards[5], ("dp", "sp"), axis=0, tiled=True),
            lax.all_gather(shards[6], ("dp", "sp"), axis=0, tiled=True),
            lax.all_gather(shards[7], ("dp", "sp"), axis=0, tiled=True),
            lax.all_gather(shards[8], ("dp", "sp"), axis=0, tiled=True),
            lax.all_gather(shards[9], ("dp", "sp"), axis=0, tiled=True),
            lax.all_gather(shards[10], ("dp", "sp"), axis=0, tiled=True),
            lax.all_gather(shards[11], ("dp", "sp"), axis=0, tiled=True),
            lax.all_gather(shards[12], ("dp", "sp"), axis=0, tiled=True),
            lax.all_gather(shards[13], ("dp", "sp"), axis=0, tiled=True),
            lax.all_gather(shards[14], ("dp", "sp"), axis=0, tiled=True),
        )
        (
            w_query,
            w_key,
            w_value,
            w_output,
            b_query,
            b_value,
            b_output,
            g_first,
            s_first,
            w_inner,
            b_inner,
            w_outer,
            b_outer,
            g_second,
            s_second,
        ) = loaded
        inputs = tokens[micro, 0]
        seg_local = doc_ids[micro, 0]
        seg_all = lax.all_gather(seg_local, "sp", axis=0, tiled=True)
        row_count, width = inputs.shape
        queries = (product(inputs, w_query) + b_query).astype(jnp.bfloat16)
        key_rows = product(inputs, w_key).astype(jnp.bfloat16)
        value_rows = (product(inputs, w_value) + b_value).astype(jnp.bfloat16)
        row_peak, row_total, summed = attend_forward(
            queries, key_rows, value_rows, seg_local, seg_all
        )
        context_heads = summed / row_total[..., None]
        log_total = row_peak + jnp.log(row_total)
        context_low = (
            jnp.transpose(context_heads, (1, 0, 2)).reshape(row_count, width).astype(jnp.bfloat16)
        )
        attended = product(context_low, w_output) + b_output
        first_out, first_normed, first_inverse = norm_forward(
            inputs.astype(jnp.float32) + attended, g_first, s_first
        )
        first_low = first_out.astype(jnp.bfloat16)
        inner = product(first_low, w_inner) + b_inner
        active = jax.nn.gelu(inner, approximate=False).astype(jnp.bfloat16)
        outer = product(active, w_outer) + b_outer
        second_out, second_normed, second_inverse = norm_forward(
            first_out + outer, g_second, s_second
        )
        results.append(second_out.astype(jnp.bfloat16))
        loaded = (
            lax.all_gather(shards[0], ("dp", "sp"), axis=0, tiled=True),
            lax.all_gather(shards[1], ("dp", "sp"), axis=0, tiled=True),
            lax.all_gather(shards[2], ("dp", "sp"), axis=0, tiled=True),
            lax.all_gather(shards[3], ("dp", "sp"), axis=0, tiled=True),
            lax.all_gather(shards[4], ("dp", "sp"), axis=0, tiled=True),
            lax.all_gather(shards[5], ("dp", "sp"), axis=0, tiled=True),
            lax.all_gather(shards[6], ("dp", "sp"), axis=0, tiled=True),
            lax.all_gather(shards[7], ("dp", "sp"), axis=0, tiled=True),
            lax.all_gather(shards[8], ("dp", "sp"), axis=0, tiled=True),
            lax.all_gather(shards[9], ("dp", "sp"), axis=0, tiled=True),
            lax.all_gather(shards[10], ("dp", "sp"), axis=0, tiled=True),
            lax.all_gather(shards[11], ("dp", "sp"), axis=0, tiled=True),
            lax.all_gather(shards[12], ("dp", "sp"), axis=0, tiled=True),
            lax.all_gather(shards[13], ("dp", "sp"), axis=0, tiled=True),
            lax.all_gather(shards[14], ("dp", "sp"), axis=0, tiled=True),
        )
        (
            w_query,
            w_key,
            w_value,
            w_output,
            b_query,
            b_value,
            b_output,
            g_first,
            s_first,
            w_inner,
            b_inner,
            w_outer,
            b_outer,
            g_second,
            s_second,
        ) = loaded
        upstream = cotangent[micro, 0].astype(jnp.float32)
        second_grad, second_gain_grad, second_shift_grad = norm_backward(
            upstream, second_normed, second_inverse, g_second
        )
        outer_grad = second_grad.astype(jnp.bfloat16)
        outer_bias_grad = jnp.sum(outer_grad.astype(jnp.float32), 0)
        outer_weight_grad = left_product(active, outer_grad)
        active_grad = right_product(outer_grad, w_outer)
        _, gelu_pull = jax.vjp(lambda hidden: jax.nn.gelu(hidden, approximate=False), inner)
        inner_grad = gelu_pull(active_grad)[0].astype(jnp.bfloat16)
        inner_bias_grad = jnp.sum(inner_grad.astype(jnp.float32), 0)
        inner_weight_grad = left_product(first_low, inner_grad)
        first_incoming = second_grad + right_product(inner_grad, w_inner)
        first_grad, first_gain_grad, first_shift_grad = norm_backward(
            first_incoming, first_normed, first_inverse, g_first
        )
        attended_grad = first_grad.astype(jnp.bfloat16)
        output_bias_grad = jnp.sum(attended_grad.astype(jnp.float32), 0)
        output_weight_grad = left_product(context_low, attended_grad)
        context_grad = right_product(attended_grad, w_output).astype(jnp.bfloat16)
        row_delta = jnp.sum(jnp.transpose(by_heads(context_grad), (1, 0, 2)) * context_heads, -1)
        query_sum, key_sum, value_sum = keys_backward(
            queries, key_rows, value_rows, context_grad, log_total, row_delta, seg_local, seg_all
        )
        query_grad = (query_sum * scaling).astype(jnp.bfloat16)
        key_grad = (key_sum * scaling).astype(jnp.bfloat16)
        value_grad = value_sum.astype(jnp.bfloat16)
        query_bias_grad = jnp.sum(query_grad.astype(jnp.float32), 0)
        value_bias_grad = jnp.sum(value_grad.astype(jnp.float32), 0)
        query_weight_grad = left_product(inputs, query_grad)
        key_weight_grad = left_product(inputs, key_grad)
        value_weight_grad = left_product(inputs, value_grad)
        input_grads.append(
            first_grad
            + right_product(query_grad, w_query)
            + right_product(key_grad, w_key)
            + right_product(value_grad, w_value)
        )
        terms = (
            query_weight_grad,
            key_weight_grad,
            value_weight_grad,
            output_weight_grad,
            query_bias_grad,
            value_bias_grad,
            output_bias_grad,
            first_gain_grad,
            first_shift_grad,
            inner_weight_grad,
            inner_bias_grad,
            outer_weight_grad,
            outer_bias_grad,
            second_gain_grad,
            second_shift_grad,
        )
        if micro == 0:
            totals = terms
        else:
            totals = tuple((earlier + latest for earlier, latest in zip(totals, terms)))
    owned = lax.psum_scatter(totals, ("dp", "sp"), scatter_dimension=0, tiled=True)
    return (
        jnp.stack(results)[:, None],
        jnp.stack(input_grads)[:, None],
        owned[0],
        owned[1],
        owned[2],
        owned[3],
        owned[4],
        owned[5],
        owned[6],
        owned[7],
        owned[8],
        owned[9],
        owned[10],
        owned[11],
        owned[12],
        owned[13],
        owned[14],
    )


def solution(mesh):
    in_specs = (
        P(None, "dp", "sp", None),
        P(None, "dp", "sp"),
        P(None, "dp", "sp", None),
        P(("dp", "sp"), None),
        P(("dp", "sp"), None),
        P(("dp", "sp"), None),
        P(("dp", "sp"), None),
        P(("dp", "sp")),
        P(("dp", "sp")),
        P(("dp", "sp")),
        P(("dp", "sp")),
        P(("dp", "sp")),
        P(("dp", "sp"), None),
        P(("dp", "sp")),
        P(("dp", "sp"), None),
        P(("dp", "sp")),
        P(("dp", "sp")),
        P(("dp", "sp")),
    )
    out_specs = (
        P(None, "dp", "sp", None),
        P(None, "dp", "sp", None),
        P(("dp", "sp"), None),
        P(("dp", "sp"), None),
        P(("dp", "sp"), None),
        P(("dp", "sp"), None),
        P(("dp", "sp")),
        P(("dp", "sp")),
        P(("dp", "sp")),
        P(("dp", "sp")),
        P(("dp", "sp")),
        P(("dp", "sp"), None),
        P(("dp", "sp")),
        P(("dp", "sp"), None),
        P(("dp", "sp")),
        P(("dp", "sp")),
        P(("dp", "sp")),
    )
    return jax.shard_map(body, mesh=mesh, in_specs=in_specs, out_specs=out_specs, check_vma=False)
```

profile of v0, /device:TPU:0, one launch (start us, length us, event | category | flops | bytes accessed | tf_op | source)
XLA Modules:
  0.0 1359.8 jit_solution(12836027228331760772)
XLA Ops:
  9.6 58.5 %all-gather.15.cloned.1.call-done = bf16[768,768]{1,0:T(8,128)(2,1)} async-done(((bf16[24,768]{1,0:T(8,128)(2,1)}), bf16[768,768]{1,0:T(8,128)(2,1)}) %all-gather.15.cloned.1.call-update) | async-done | bytes 1179664 | tf_op jit(solution)/shard_map/all_gather | solution.py:160
  72.8 39.6 %all-reduce.19 = (bf16[3072]{0:T(1024)(128)(2,1)S(1)}, bf16[768]{0:T(1024)(128)(2,1)S(1)}, bf16[768]{0:T(1024)(128)(2,1)S(1)}, bf16[768]{0:T(1024)(128)(2,1)S(1)...) all-reduce(bf16[3072]{0:T(1024)(128)(2,1)S(1)} %dynamic-update-slic, ...), channel_id=1, replica_groups=mesh['dp'=4,'sp'=8] {'dp','sp'}, use_global_device_ids=true, to_apply=%add.5 | all-reduce | flops 9216 | bytes 36864
  112.4 11.9 all-gather.19.cloned.1.call-done
  131.2 10.5 all-gather
  141.7 8.8 all-gather.1
  150.8 29.7 %all-gather.13.cloned.1.call-done = bf16[768,768]{1,0:T(8,128)(2,1)} async-done(((bf16[24,768]{1,0:T(8,128)(2,1)}), bf16[768,768]{1,0:T(8,128)(2,1)}) %all-gather.13.cloned.1.call-update) | async-done | bytes 1179664 | tf_op jit(solution)/shard_map/all_gather | solution.py:159
  182.8 23.7 %all-gather.17.cloned.1.call-done = bf16[1024,768]{1,0:T(8,128)(2,1)} async-done(((bf16[128,768]{1,0:T(8,128)(2,1)}), bf16[1024,768]{1,0:T(8,128)(2,1)}) %all-gather.17.cloned.1.call-update) | async-done | bytes 1572880 | tf_op jit(solution)/shard_map/all_gather | solution.py:56
  208.3 25.0 %all-gather.21.cloned.1.call-done = bf16[1024,768]{1,0:T(8,128)(2,1)} async-done(((bf16[128,768]{1,0:T(8,128)(2,1)}), bf16[1024,768]{1,0:T(8,128)(2,1)}) %all-gather.21.cloned.1.call-update) | async-done | bytes 1572880 | tf_op jit(solution)/shard_map/all_gather | solution.py:57
  235.8 24.1 %all-gather.29.cloned.1.call-done = bf16[1024,768]{1,0:T(8,128)(2,1)} async-done(((bf16[128,768]{1,0:T(8,128)(2,1)}), bf16[1024,768]{1,0:T(8,128)(2,1)}) %all-gather.29.cloned.1.call-update) | async-done | bytes 1572880 | tf_op jit(solution)/shard_map/all_gather | solution.py:56
  262.5 24.2 %all-gather.31.cloned.1.call-done = bf16[1024,768]{1,0:T(8,128)(2,1)} async-done(((bf16[128,768]{1,0:T(8,128)(2,1)}), bf16[1024,768]{1,0:T(8,128)(2,1)}) %all-gather.31.cloned.1.call-update) | async-done | bytes 1572880 | tf_op jit(solution)/shard_map/all_gather | solution.py:57
  296.0 47.6 %all-gather.23.cloned.1.call-done = bf16[768,768]{1,0:T(8,128)(2,1)} async-done(((bf16[24,768]{1,0:T(8,128)(2,1)}), bf16[768,768]{1,0:T(8,128)(2,1)}) %all-gather.23.cloned.1.call-update) | async-done | bytes 1179664 | tf_op jit(solution)/shard_map/all_gather | solution.py:162
  353.6 55.6 %all-gather.25.cloned.1.call-done = bf16[768,3072]{1,0:T(8,128)(2,1)} async-done(((bf16[24,3072]{1,0:T(8,128)(2,1)}), bf16[768,3072]{1,0:T(8,128)(2,1)}) %all-gather.25.cloned.1.call-update) | async-done | bytes 4718608 | tf_op jit(solution)/shard_map/all_gather | solution.py:168
  409.2 8.8 multiply_convert_fusion.3
  418.0 56.6 %all-gather.27.cloned.1.call-done = bf16[3072,768]{1,0:T(8,128)(2,1)} async-done(((bf16[96,768]{1,0:T(8,128)(2,1)}), bf16[3072,768]{1,0:T(8,128)(2,1)}) %all-gather.27.cloned.1.call-update) | async-done | bytes 4718608 | tf_op jit(solution)/shard_map/all_gather | solution.py:170
  474.6 3.4 fusion.147
  478.3 4.1 multiply_convert_fusion.2
  502.0 4.4 fusion.8
  510.8 3.2 pad_maximum_fusion
  520.8 5.9 multiply_convert_fusion
  529.9 3.3 pad_maximum_fusion.1
  534.6 3.3 convert_reduce_fusion.11
  553.0 5.2 convolution_add_fusion.1
  560.9 5.1 convolution_add_fusion
  566.1 16.8 %reduce-scatter.15.cloned.1.call-done = f32[128,1536]{0,1:T(8,128)} async-done(((f32[1024,1536]{0,1:T(8,128)}), f32[128,1536]{0,1:T(8,128)}) %reduce-scatter.15.cloned.1.call-update) | async-done | bytes 786448 | tf_op jit(solution)/shard_map/reduce_scatter | solution.py:111
  584.3 68.9 %reduce-scatter.17.cloned.1.call-done = f32[128,1536]{0,1:T(8,128)} async-done(((f32[1024,1536]{0,1:T(8,128)}), f32[128,1536]{0,1:T(8,128)}) %reduce-scatter.17.cloned.1.call-update) | async-done | bytes 786448 | tf_op jit(solution)/shard_map/reduce_scatter | solution.py:111
  675.2 39.1 %all-reduce.18 = (f32[768]{0:T(1024)S(1)}, f32[768]{0:T(1024)S(1)}, f32[768]{0:T(1024)S(1)}, f32[768]{0:T(1024)S(1)}, f32[768]{0:T(1024)S(1)}, /*index=5*/f32[30...) all-reduce(f32[768]{0:T(1024)} %add.318, ...), channel_id=10, replica_groups=mesh['dp'=4,'sp'=8] {'dp','sp'}, use_global_device_ids=true, to_apply=%region_30.31.clone | all-reduce | flops 9216 | bytes 73728
  724.2 32.6 %reduce-scatter.25.cloned.1.call-done = f32[24,768]{1,0:T(8,128)} async-done(((f32[768,768]{1,0:T(8,128)}), f32[24,768]{1,0:T(8,128)}) %reduce-scatter.25.cloned.1.call-update) | async-done | bytes 73744
  756.9 104.6 %reduce-scatter.19.cloned.1.call-done = f32[24,768]{1,0:T(8,128)} async-done(((f32[768,768]{1,0:T(8,128)}), f32[24,768]{1,0:T(8,128)}) %reduce-scatter.19.cloned.1.call-update) | async-done | bytes 73744 | tf_op jit(solution)/shard_map/reduce_scatter | solution.py:312
  861.5 141.0 %reduce-scatter.21.cloned.1.call-done = f32[24,3072]{1,0:T(8,128)} async-done(((f32[768,3072]{1,0:T(8,128)}), f32[24,3072]{1,0:T(8,128)}) %reduce-scatter.21.cloned.1.call-update) | async-done | bytes 294928 | tf_op jit(solution)/shard_map/reduce_scatter | solution.py:312
  1002.5 141.8 %reduce-scatter.23.cloned.1.call-done = f32[96,768]{1,0:T(8,128)} async-done(((f32[3072,768]{1,0:T(8,128)}), f32[96,768]{1,0:T(8,128)}) %reduce-scatter.23.cloned.1.call-update) | async-done | bytes 294928 | tf_op jit(solution)/shard_map/reduce_scatter | solution.py:312
  1144.3 103.7 %reduce-scatter.27.cloned.1.call-done = f32[24,768]{1,0:T(8,128)} async-done(((f32[768,768]{1,0:T(8,128)}), f32[24,768]{1,0:T(8,128)}) %reduce-scatter.27.cloned.1.call-update) | async-done | bytes 73744
  1248.1 104.6 %reduce-scatter.29.cloned.1.call-done = f32[24,768]{1,0:T(8,128)} async-done(((f32[768,768]{1,0:T(8,128)}), f32[24,768]{1,0:T(8,128)}) %reduce-scatter.29.cloned.1.call-update) | async-done | bytes 73744
  (391 shorter events, 128.2 us)
Async XLA Ops:
  7.2 117.2 %copy-start.2 = (bf16[2,1,128,768]{3,2,1,0:T(8,128)(2,1)S(1)}, bf16[2,1,128,768]{3,2,1,0:T(8,128)(2,1)}, u32[]{:S(2)}) copy-start(bf16[2,1,128,768]{3,2,1,0:T(8,128)(2,1)} %param.18) | copy-start | bytes 1179652
  7.2 64.1 %copy-start.95 = (bf16[24]{0:T(256)(128)(2,1)S(1)}, bf16[24]{0:T(256)(128)(2,1)}, u32[]{:S(2)}) copy-start(bf16[24]{0:T(256)(128)(2,1)} %param.29) | copy-start | bytes 148
  7.2 64.3 %copy-start.96 = (bf16[24]{0:T(256)(128)(2,1)S(1)}, bf16[24]{0:T(256)(128)(2,1)}, u32[]{:S(2)}) copy-start(bf16[24]{0:T(256)(128)(2,1)} %param.28) | copy-start | bytes 148
  7.3 64.6 %copy-start.97 = (bf16[24]{0:T(256)(128)(2,1)S(1)}, bf16[24]{0:T(256)(128)(2,1)}, u32[]{:S(2)}) copy-start(bf16[24]{0:T(256)(128)(2,1)} %param.33) | copy-start | bytes 148
  7.3 64.8 %copy-start.98 = (bf16[24]{0:T(256)(128)(2,1)S(1)}, bf16[24]{0:T(256)(128)(2,1)}, u32[]{:S(2)}) copy-start(bf16[24]{0:T(256)(128)(2,1)} %param.35) | copy-start | bytes 148
  7.3 65.0 %copy-start.99 = (bf16[24]{0:T(256)(128)(2,1)S(1)}, bf16[24]{0:T(256)(128)(2,1)}, u32[]{:S(2)}) copy-start(bf16[24]{0:T(256)(128)(2,1)} %param.34) | copy-start | bytes 148
  7.3 65.2 %copy-start.100 = (bf16[96]{0:T(256)(128)(2,1)S(1)}, bf16[96]{0:T(256)(128)(2,1)}, u32[]{:S(2)}) copy-start(bf16[96]{0:T(256)(128)(2,1)} %param.31) | copy-start | bytes 580
  7.3 60.8 %all-gather.15.cloned.1.call-start = ((), (), s32[]{:S(2)}) async-start(), calls=%async_computation.9 | async-start | bytes 1216512 | tf_op jit(solution)/shard_map/all_gather | solution.py:160
  8.0 116.3 %all-gather.19.cloned.1.call-start = ((), (), s32[]{:S(2)}) async-start(), calls=%async_computation.11 | async-start | bytes 1216512 | tf_op jit(solution)/shard_map/all_gather | solution.py:161
  8.8 171.7 %all-gather.13.cloned.1.call-start = ((), (), s32[]{:S(2)}) async-start(), calls=%async_computation.8 | async-start | bytes 1216512 | tf_op jit(solution)/shard_map/all_gather | solution.py:159
  9.5 197.0 %all-gather.17.cloned.1.call-start = ((), (), s32[]{:S(2)}) async-start(), calls=%async_computation.10 | async-start | bytes 1769472 | tf_op jit(solution)/shard_map/all_gather | solution.py:56
  70.6 162.7 %all-gather.21.cloned.1.call-start = ((), (), s32[]{:S(2)}) async-start(), calls=%async_computation.12 | async-start | bytes 1769472 | tf_op jit(solution)/shard_map/all_gather | solution.py:57
  126.7 133.2 %all-gather.29.cloned.1.call-start = ((), (), s32[]{:S(2)}) async-start(), calls=%async_computation.16 | async-start | bytes 1769472 | tf_op jit(solution)/shard_map/all_gather | solution.py:56
  127.8 158.9 %all-gather.31.cloned.1.call-start = ((), (), s32[]{:S(2)}) async-start(), calls=%async_computation.17 | async-start | bytes 1769472 | tf_op jit(solution)/shard_map/all_gather | solution.py:57
  128.9 214.6 %all-gather.23.cloned.1.call-start = ((), (), s32[]{:S(2)}) async-start(), calls=%async_computation.13 | async-start | bytes 1216512 | tf_op jit(solution)/shard_map/all_gather | solution.py:162
  129.7 279.5 %all-gather.25.cloned.1.call-start = ((), (), s32[]{:S(2)}) async-start(), calls=%async_computation.14 | async-start | bytes 4866048 | tf_op jit(solution)/shard_map/all_gather | solution.py:168
  130.4 344.1 %all-gather.27.cloned.1.call-start = ((), (), s32[]{:S(2)}) async-start(), calls=%async_computation.15 | async-start | bytes 4866048 | tf_op jit(solution)/shard_map/all_gather | solution.py:170
  131.0 451.9 %reduce-scatter.15.cloned.1.call-start = ((), (), s32[]{:S(2)}) async-start(), calls=%async_computation.18 | async-start | bytes 7077888 | tf_op jit(solution)/shard_map/reduce_scatter | solution.py:111
  182.3 107.0 %copy-start.47 = (bf16[128,768]{0,1:T(8,128)(2,1)}, bf16[128,768]{0,1:T(8,128)(2,1)S(1)}, u32[]{:S(2)}) copy-start(bf16[128,768]{0,1:T(8,128)(2,1)S(1)} %copy.67) | copy-start | bytes 589828
  182.8 162.6 %copy-start.45 = (bf16[128,768]{0,1:T(8,128)(2,1)}, bf16[128,768]{0,1:T(8,128)(2,1)S(1)}, u32[]{:S(2)}) copy-start(bf16[128,768]{0,1:T(8,128)(2,1)S(1)} %copy.70) | copy-start | bytes 589828
  208.3 81.1 %copy-start.13 = (bf16[1024,768]{0,1:T(8,128)(2,1)}, bf16[1024,768]{0,1:T(8,128)(2,1)S(1)}, u32[]{:S(2)}) copy-start(bf16[1024,768]{0,1:T(8,128)(2,1)S(1)} %copy.68) | copy-start | bytes 4718596
  345.3 148.5 %copy-start.68 = (f32[128]{0:T(128)}, f32[128]{0:T(128)S(1)}, u32[]{:S(2)}) copy-start(f32[128]{0:T(128)S(1)} %broadcast_multiply_fusion.11) | copy-start | bytes 1540
  352.8 141.0 %copy-start.81 = (f32[128]{0:T(128)}, f32[128]{0:T(128)S(1)}, u32[]{:S(2)}) copy-start(f32[128]{0:T(128)S(1)} %broadcast_multiply_fusion.9) | copy-start | bytes 1540
  353.0 140.8 %copy-start.83 = (f32[128]{0:T(128)}, f32[128]{0:T(128)S(1)}, u32[]{:S(2)}) copy-start(f32[128]{0:T(128)S(1)} %add_rsqrt_fusion.3) | copy-start | bytes 1540
  353.0 140.8 %copy-start.87 = (f32[128]{0:T(128)}, f32[128]{0:T(128)S(1)}, u32[]{:S(2)}) copy-start(f32[128]{0:T(128)S(1)} %add_rsqrt_fusion.1) | copy-start | bytes 1540
  514.1 139.2 %reduce-scatter.17.cloned.1.call-start = ((), (), s32[]{:S(2)}) async-start(), calls=%async_computation.19 | async-start | bytes 7077888 | tf_op jit(solution)/shard_map/reduce_scatter | solution.py:111
  533.2 223.6 %reduce-scatter.25.cloned.1.call-start = ((), (), s32[]{:S(2)}) async-start(), calls=%async_computation.23 | async-start | bytes 2433024
  547.0 314.4 %reduce-scatter.19.cloned.1.call-start = ((), (), s32[]{:S(2)}) async-start(), calls=%async_computation.20 | async-start | bytes 2433024 | tf_op jit(solution)/shard_map/reduce_scatter | solution.py:312
  550.4 452.1 %reduce-scatter.21.cloned.1.call-start = ((), (), s32[]{:S(2)}) async-start(), calls=%async_computation.21 | async-start | bytes 9732096 | tf_op jit(solution)/shard_map/reduce_scatter | solution.py:312
  558.3 586.1 %reduce-scatter.23.cloned.1.call-start = ((), (), s32[]{:S(2)}) async-start(), calls=%async_computation.22 | async-start | bytes 9732096 | tf_op jit(solution)/shard_map/reduce_scatter | solution.py:312
  566.0 682.1 %reduce-scatter.27.cloned.1.call-start = ((), (), s32[]{:S(2)}) async-start(), calls=%async_computation.24 | async-start | bytes 2433024
  659.3 693.4 %reduce-scatter.29.cloned.1.call-start = ((), (), s32[]{:S(2)}) async-start(), calls=%async_computation.25 | async-start | bytes 2433024
  (95 other events, 825.9 us)
Sparse Core Ops, SparseCore 0:
  11.1 56.8 all-gather.14
  71.1 53.2 all-gather.18
  127.4 53.0 all-gather.12
  182.5 23.9 all-gather.16
  208.6 24.5 all-gather.20
  235.3 24.5 all-gather.28
  262.1 24.5 all-gather.30
  289.8 53.7 all-gather.22
  346.6 62.5 all-gather.24
  412.1 62.4 all-gather.26
  514.2 68.6 reduce-scatter.14
  585.0 68.1 reduce-scatter.16
  659.1 97.7 reduce-scatter.24
  763.4 97.9 reduce-scatter.18
  867.8 134.6 reduce-scatter.20
  1009.8 134.4 reduce-scatter.22
  1150.0 97.9 reduce-scatter.26
  1254.6 97.9 reduce-scatter.28
where the time goes:
time: 1370 us; the launch traced here: 1360 us
  waiting for transfers between devices  1080 us (79%)
  matrix products  99.7 us (7%)
  blocking collectives  98 us (7%)
  local copies, waits for them, and re-layouts  45.4 us (3%)
  other arithmetic  24.7 us (2%)
  between operations  15.8 us (1%)
    reduce_scatter x3, waiting for transfers between devices, body(): lax.psum_scatter(totals, ('dp', 'sp'), scatter_dimension=0, tiled=True)  387 us
    unnamed x21, waiting for transfers between devices  245 us
    reduce_scatter x2, waiting for transfers between devices, keys_backward(): lax.psum_scatter(pair_sum, 'sp', scatter_dimension=0, tiled=True)  85.7 us
    unnamed x2, blocking collectives  78.7 us
    all_gather x1, waiting for transfers between devices, body(): lax.all_gather(shards[1], ('dp', 'sp'), axis=0, tiled=True)  58.5 us
    all_gather x1, waiting for transfers between devices, body(): lax.all_gather(shards[11], ('dp', 'sp'), axis=0, tiled=True)  56.6 us
    all_gather x1, waiting for transfers between devices, body(): lax.all_gather(shards[9], ('dp', 'sp'), axis=0, tiled=True)  55.6 us
    all_gather x2, waiting for transfers between devices, attend_forward(): value_piece = lax.all_gather(value_rows, 'sp', axis=0, tiled=True)  49.2 us
  transfers between devices with their start and end apart: 18, of which 18 were waited for; matrix products, arithmetic and copies ran while one was open for 9% of the time, Pallas kernels for 0%

commit v1 on v0

--- a/solution.py
+++ b/solution.py
@@ -1,6 +1,10 @@
+import functools
+
 import jax
 import jax.numpy as jnp
 from jax import lax
+from jax.experimental import pallas as pl
+from jax.experimental.pallas import tpu as pltpu
 from jax.sharding import PartitionSpec as P
 
 HEADS = 12
@@ -113,7 +117,7 @@
     return (query_sum, pair_mine[:, :width], pair_mine[:, width:])
 
 
-def body(
+def body_general(
     tokens,
     doc_ids,
     cotangent,
@@ -331,7 +335,818 @@
     )
 
 
+BIT_Y, BIT_X, BIT_ZH, BIT_ZL, BIT_C = 16, 8, 4, 2, 1
+AXES = ("dp", "sp")
+GAUSS = 0.3989422804014327
+LIMITS = {
+    "first": 2, "query": 2, "attend": 16, "forward": 20, "outer_grad": 12, "middle": 20, "inner_grad": 12,
+    "attend_back": 20, "attend_weight": 14,
+}
+SIDE = 64
+SCALE = 0.0
+DOC_ROWS = 16
+BF16, F32 = jnp.bfloat16, jnp.float32
+
+
+def low(array):
+    return array.astype(BF16)
+
+
+def swap(array, mask):
+    return lax.ppermute(array, AXES, [(i, i ^ mask) for i in range(32)])
+
+
+class Turns:
+    def __init__(self):
+        self.last = None
+
+    def __call__(self, array):
+        if self.last is not None:
+            array, _ = lax.optimization_barrier((array, self.last))
+        self.last = array
+        return array
+
+
+def tie(array, other):
+    return lax.optimization_barrier((array, other))[0]
+
+
+def join(bit, own, other, axis=0):
+    return jnp.where(
+        bit == 0, jnp.concatenate([own, other], axis), jnp.concatenate([other, own], axis)
+    )
+
+
+def pair(own, other):
+    return jnp.concatenate([own, other], 0)
+
+
+def add_low(own, other):
+    return low(own.astype(F32) + other.astype(F32))
+
+
+def call(kernel, outs, operands, spaces=None, scratch=(), flops=0, traffic=0, name=None):
+    whole = pl.BlockSpec(memory_space=pltpu.VMEM)
+    specs = [pl.BlockSpec(memory_space=pltpu.SMEM)]
+    operands = list(operands)
+    for n, kind in enumerate(spaces or ["vmem"] * (len(operands) - 1), 1):
+        specs.append(whole if kind == "vmem" else pl.BlockSpec(memory_space=pltpu.HBM))
+        if kind == "hbm":
+            operands[n] = pltpu.with_memory_space_constraint(operands[n], pltpu.HBM)
+    return pl.pallas_call(
+        kernel,
+        out_shape=tuple(jax.ShapeDtypeStruct(shape, dtype) for shape, dtype in outs),
+        in_specs=specs,
+        out_specs=tuple(whole for _ in outs),
+        scratch_shapes=list(scratch),
+        compiler_params=pltpu.CompilerParams(vmem_limit_bytes=LIMITS[name] * 1024 * 1024),
+        cost_estimate=pl.CostEstimate(flops=int(flops * SCALE) + 1, transcendentals=0, bytes_accessed=int(traffic * SCALE) + 1),
+        name=name,
+    )(*operands)
+
+
+def block_at(place, k):
+    return (place[0] ^ (k // 2)) * 2 + (place[1] ^ (k % 2))
+
+
+def unit_at(place, u):
+    return (place[2] ^ (u // 2)) * 2 + (place[3] ^ (u % 2))
+
+
+def first_kernel(place, tokens, docs, inner, outer, output, x_keep, x_give, keep, give, ids, sems):
+    zh, c = place[2], place[4]
+    rows, width = tokens.shape[1:]
+    shard, cols = keep.shape[1:]
+    started = [pltpu.make_async_copy(docs, ids, sems.at[0])]
+    for flip in range(2):
+        x_out, out = (x_keep, x_give)[flip], (keep, give)[flip]
+        moves = [(tokens.at[zh ^ flip], x_out.at[pl.ds(0, rows), :])]
+        half = c ^ flip
+        for j in range(4):
+            at = pl.ds(pl.multiple_of(half * (4 * cols) + j * cols, 128), cols)
+            moves.append((inner.at[:, at], out.at[j]))
+        at = pl.ds(pl.multiple_of(half * cols, 128), cols)
+        for j in range(4):
+            moves.append((outer.at[pl.ds(shard * j, shard), at], out.at[4 + j]))
+        moves.append((output.at[:, at], out.at[8]))
+        for source, target in moves:
+            started.append(pltpu.make_async_copy(source, target, sems.at[len(started)]))
+    for copy in started:
+        copy.start()
+    for copy in started:
+        copy.wait()
+    for flip, out in ((0, x_keep), (1, x_give)):
+        line = ids[pl.ds(zh ^ flip, 1), :].astype(F32)
+        line = jnp.concatenate([line, jnp.zeros((1, width - rows), F32)], 1)
+        out[rows : rows + DOC_ROWS, :] = low(jnp.broadcast_to(line, (DOC_ROWS, width)))
+
+
+def query_kernel(place, wq, wk, wv, smalls, q_keep, q_give, weights, blocks, side, sems):
+    zl, c = place[3], place[4]
+    shard, width = wq.shape
+    cut = width // 4
+    started = [
+        pltpu.make_async_copy(w, weights.at[n], sems.at[n]) for n, w in enumerate((wq, wk, wv))
+    ]
+    for copy in started:
+        copy.start()
+    side[...] = jnp.zeros_like(side)
+    side[SIDE : SIDE + 16, :] = smalls[...]
+    columns = low(jnp.transpose(side[...]))[:shard, SIDE:]
+    for copy in started:
+        copy.wait()
+    for p in range(4):
+        at = slice(cut * p, cut * (p + 1))
+        blocks[p] = jnp.concatenate([weights[0, :, at], weights[1, :, at], weights[2, :, at], columns], 1)
+    for r in range(2):
+        q_keep[r] = blocks[2 * (zl ^ r) + c]
+        q_give[r] = blocks[2 * (zl ^ r) + (1 - c)]
+
+
+def attend_kernel(place, w0, w1, w2, w3, x_own, x_other, *refs):
+    outs, (w, doc_col) = refs[:-2], refs[-2:]
+    context_out, (queries_out, keys_out, values_out, wide_out, lse_out, vec_out, doc_out) = (
+        outs[:2], outs[2:],
+    )
+    cut = queries_out.shape[1]
+    heads = cut // HEAD
+    size = w0.shape[1]
+    for k, part in enumerate((w0, w1, w2, w3)):
+        for u in range(4):
+            at = block_at(place, k) * (4 * size) + unit_at(place, u) * size
+            w[pl.ds(pl.multiple_of(at, 16), size), :] = part[u]
+    group = place[5]
+    tile = slice(3 * cut - SIDE, 3 * cut + SIDE)
+    vec_out[...] = jnp.transpose(w[:, tile].astype(F32))[SIDE : SIDE + 16, :]
+    biases = w[pl.ds(pl.multiple_of(group * cut, 64), cut), tile].astype(F32)
+    biases = jnp.transpose(jnp.concatenate([biases, jnp.zeros((64, 2 * SIDE), F32)], 0))
+    bq, bv = biases[SIDE : SIDE + 1, :cut], biases[SIDE + 1 : SIDE + 2, :cut]
+    rows = x_own.shape[1] - DOC_ROWS
+    ids = []
+    for n in range(8):
+        source = (x_own, x_other)[n // 4]
+        part = product(source[n % 4, 0:rows, :], w[:, : 3 * cut])
+        at = pl.ds(rows * n, rows)
+        queries_out[at, :] = low(part[:, :cut] + bq)
+        keys_out[at, :] = low(part[:, cut : 2 * cut])
+        values_out[at, :] = low(part[:, 2 * cut :] + bv)
+        ids.append(source[n % 4, rows : rows + 1, 0:128].astype(F32))
+    doc_row = jnp.concatenate(ids, 1)
+    doc_out[...] = jnp.broadcast_to(doc_row, doc_out.shape)
+    turned = jnp.transpose(jnp.concatenate(ids + [jnp.zeros((120, 128), F32)], 0))
+    for n in range(8):
+        doc_col[pl.ds(rows * n, rows), :] = jnp.broadcast_to(turned[:, n : n + 1], (rows, 128))
+    rows = 2 * rows
+    lane = lax.broadcasted_iota(jnp.int32, (rows, 128), 1)
+    for i in (2, 3, 0, 1):
+        at = pl.ds(rows * i, rows)
+        same = doc_col[at, 0:1] == doc_row
+        pieces = []
+        logs = jnp.zeros((rows, 128), F32)
+        for h in range(heads):
+            cols = slice(HEAD * h, HEAD * (h + 1))
+            query = queries_out[at, cols] * BF16(HEAD**-0.5)
+            scores = right_product(query, keys_out[:, cols])
+            scores = jnp.where(same, scores, NEG)
+            peak = jnp.max(scores, -1, keepdims=True)
+            weights = jnp.exp(scores - peak)
+            denom = jnp.sum(weights, -1, keepdims=True)
+            summed = product(low(weights), values_out[:, cols])
+            pieces.append(summed / denom)
+            logs = jnp.where(lane == h, peak + jnp.log(denom), logs)
+        context = jnp.concatenate(pieces, 1)
+        wide_out[at, :] = context
+        context_out[i // 2][i % 2] = low(context)
+        lse_out[:, at] = jnp.transpose(logs)[:8, :]
+
+
+def attend_back_kernel(
+    place, q, k, v, wide, lse, g0, g1, g2, g3, docs, grads, sums, dq_acc, delta_ref, dc, doc_col
+):
+    total, cut = q.shape
+    heads = cut // HEAD
+    rows = total // 4
+    scaling = HEAD**-0.5
+    lane = lax.broadcasted_iota(jnp.int32, (rows, 128), 1)
+    doc_row = docs[0:1, :]
+    for n in range(total // 128):
+        at = slice(128 * n, 128 * (n + 1))
+        turned = jnp.transpose(jnp.broadcast_to(docs[0:1, at], (128, 128)))
+        doc_col[at, :] = turned
+    for i, g in enumerate((g0, g1, g2, g3)):
+        at = pl.ds(rows * i, rows)
+        grad = g[...]
+        dc[at, :] = grad
+        prod = grad.astype(F32) * wide[at, :]
+        cols = jnp.zeros((rows, 128), F32)
+        for h in range(heads):
+            piece = jnp.sum(prod[:, HEAD * h : HEAD * (h + 1)], -1, keepdims=True)
+            cols = jnp.where(lane == h, piece, cols)
+        delta_ref[:, at] = jnp.transpose(cols)[:8, :]
+    for h in range(heads):
+        cols = slice(HEAD * h, HEAD * (h + 1))
+        query = q[:, cols]
+        scaled = query * BF16(scaling)
+        grad_rows = dc[:, cols]
+        for i in range(4):
+            at = pl.ds(rows * i, rows)
+            key = k[at, cols]
+            value = v[at, cols]
+            same = doc_col[at, 0:1] == doc_row
+            scores = jnp.where(same, right_product(key, scaled), NEG)
+            probs = jnp.exp(scores - lse[h : h + 1, :])
+            prob_grad = right_product(value, grad_rows)
+            score_grad = low(probs * (prob_grad - delta_ref[h : h + 1, :]))
+            grads[at, cut + HEAD * h : cut + HEAD * (h + 1)] = low(product(score_grad, query) * scaling)
+            grads[at, 2 * cut + HEAD * h : 2 * cut + HEAD * (h + 1)] = low(product(low(probs), grad_rows))
+            piece = left_product(key, score_grad)
+            if i == 0:
+                dq_acc[...] = piece
+            else:
+                dq_acc[...] += piece
+        grads[:, cols] = low(jnp.transpose(dq_acc[...]) * scaling)
+    grads[:, 3 * cut :] = jnp.zeros((total, SIDE), BF16)
+    sums[0:1, :] = jnp.sum(grads[...].astype(F32), 0, keepdims=True)
+
+
+def attend_weight_kernel(order, place, x_own, x_other, grads, w0, w1, w2, w3, sums, extra, *refs):
+    outs, input_outs, (turned, w, side) = refs[:4], refs[4:7], refs[7:]
+    rows = x_own.shape[1] - DOC_ROWS
+    group = place[5]
+    cut = extra.shape[1] // 4
+    for n in range(8):
+        source = (x_own, x_other)[n // 4]
+        turned[:, pl.ds(rows * n, rows)] = jnp.transpose(source[n % 4, 0:rows, :])
+    size = w0.shape[1]
+    for k, part in enumerate((w0, w1, w2, w3)):
+        for u in range(4):
+            at = block_at(place, k) * (4 * size) + unit_at(place, u) * size
+            w[pl.ds(pl.multiple_of(at, 16), size), :] = part[u]
+    width = extra.shape[1]
+    pad = jnp.concatenate([jnp.zeros((SIDE + 2, width), F32), extra[...], jnp.zeros((SIDE - 18, width), F32)], 0)
+    side[...] = jnp.transpose(pad)
+    own = jnp.concatenate([sums[0:1, :cut], sums[0:1, 2 * cut : 3 * cut]], 0)
+    own = jnp.concatenate([own, jnp.zeros((2, 256 - cut), F32)], 1)
+    own = jnp.concatenate([jnp.zeros((SIDE, 256), F32), own, jnp.zeros((SIDE - 2, 256), F32)], 0)
+    at = pl.ds(pl.multiple_of(group * cut, 64), cut)
+    side[at, :] += jnp.transpose(own)[:cut, :]
+    for n, k in enumerate(order):
+        at = pl.ds(pl.multiple_of(block_at(place, k) * (4 * size), 64), 4 * size)
+        piece = product(turned[at, :], grads[...])
+        piece = jnp.concatenate([piece[:, : 3 * cut - SIDE], piece[:, 3 * cut - SIDE :] + side[at, :]], 1)
+        for a in range(4):
+            outs[n][unit_at(place, a)] = low(piece[size * a : size * (a + 1), :])
+    for n in (2, 3, 1, 0):
+        at = pl.ds(2 * rows * n, 2 * rows)
+        part = right_product(grads[at, : 3 * cut], w[:, : 3 * cut])
+        if n == 0:
+            input_outs[0][...] = part
+        elif n == 1:
+            input_outs[1][...] = low(part)
+        else:
+            input_outs[2][n - 2] = low(part)
+
+
+def copies(pieces, whole, place, sems, base, column_blocks, first, row_count):
+    c = place[4]
+    started = []
+    for half in range(2):
+        for k in range(4):
+            for u in range(4):
+                for j in range(column_blocks):
+                    source = pieces[half * 4 + k]
+                    cols = source.shape[-1]
+                    row = block_at(place, k) * (4 * row_count) + unit_at(place, u) * row_count
+                    col = (c ^ half) * (column_blocks * cols) + j * cols
+                    target = whole.at[
+                        pl.ds(pl.multiple_of(row, 16), row_count), pl.ds(pl.multiple_of(col, 128), cols)
+                    ]
+                    if column_blocks > 1:
+                        source = source.at[u, j]
+                    else:
+                        source = source.at[u, pl.ds(first, row_count), :]
+                    started.append(pltpu.make_async_copy(source, target, sems.at[base + len(started)]))
+    return started
+
+
+def forward_kernel(place, c0, c1, c2, c3, x_ref, vec, b_inner, *refs):
+    a_p, b_p = refs[:8], refs[8:16]
+    (out, n2_out, r2_out, h1b_out, n1_out, r1_out, g_out, gp_out) = refs[16:24]
+    wo, wi, wu, sems = refs[24:]
+    unit = wo.shape[0] // 16
+    copy_o = copies(b_p, wo, place, sems, 0, 1, 4 * unit, unit)
+    copy_i = copies(a_p, wi, place, sems, 32, 4, 0, unit)
+    copy_u = copies(b_p, wu, place, sems, 160, 1, 0, 4 * unit)
+    for copy in copy_o + copy_i + copy_u:
+        copy.start()
+    group = place[5]
+    rows = x_ref.shape[1] - DOC_ROWS
+    cut = c0.shape[-1]
+    for copy in copy_o:
+        copy.wait()
+    attended = vec[2:3, :]
+    for mask, part in enumerate((c0, c1, c2, c3)):
+        at = pl.ds(pl.multiple_of((group ^ mask) * cut, 64), cut)
+        attended = attended + product(part[...], wo[at, :])
+    tokens = jnp.concatenate([x_ref[0, 0:rows, :], x_ref[1, 0:rows, :]], 0)
+    first_out, normed, inverse = norm_forward(tokens.astype(F32) + attended, vec[3:4, :], vec[4:5, :])
+    n1_out[...] = normed
+    r1_out[...] = jnp.broadcast_to(inverse, r1_out.shape)
+    h1b_out[...] = low(first_out)
+    for copy in copy_i + copy_u:
+        copy.wait()
+    outer = vec[5:6, :]
+    step = 512
+    for j in range(wi.shape[1] // step):
+        at = slice(step * j, step * (j + 1))
+        hidden = product(h1b_out[...], wi[:, at]) + b_inner[:, at]
+        half = 0.5 + 0.5 * lax.erf(hidden * (0.5**0.5))
+        active = low(hidden * half)
+        g_out[:, at] = active
+        gp_out[:, at] = half + hidden * jnp.exp(hidden * hidden * -0.5) * GAUSS
+        outer = outer + product(active, wu[at, :])
+    second_out, normed, inverse = norm_forward(first_out + outer, vec[6:7, :], vec[7:8, :])
+    out[...] = low(second_out)
+    n2_out[...] = normed
+    r2_out[...] = jnp.broadcast_to(inverse, r2_out.shape)
+
+
+def outer_grad_kernel(
+    place, cot_own, cot_other, n2, r2, vec, g_ref, give, keep, dz2_out, df_ref, sums
+):
+    c = place[4]
+    upstream = jnp.concatenate([cot_own[...], cot_other[...]], 0).astype(F32)
+    grad, gain_grad, shift_grad = norm_backward(upstream, n2[...], r2[:, 0:1], vec[6:7, :])
+    dz2_out[...] = grad
+    grad_low = low(grad)
+    df_ref[...] = grad_low
+    sums[0:1, :] = gain_grad[None]
+    sums[1:2, :] = shift_grad[None]
+    sums[2:3, :] = jnp.sum(grad_low.astype(F32), 0, keepdims=True)
+    unit, cols = give.shape[2:]
+    give_part = df_ref[:, pl.ds(pl.multiple_of((1 - c) * cols, 128), cols)]
+    keep_part = df_ref[:, pl.ds(pl.multiple_of(c * cols, 128), cols)]
+    both = jnp.concatenate([give_part, keep_part], 1)
+    for k in range(4):
+        at = pl.ds(pl.multiple_of(block_at(place, k) * (4 * unit), 128), 4 * unit)
+        piece = low(left_product(g_ref[:, at], both))
+        for a in range(4):
+            at = slice(unit * a, unit * (a + 1))
+            give[k, unit_at(place, a)] = piece[at, :cols]
+            keep[k, unit_at(place, a)] = piece[at, cols:]
+
+
+def middle_kernel(place, df_ref, gp_ref, dz2, n1, r1, vec, *refs):
+    a_p, b_p = refs[:8], refs[8:16]
+    du, grad_out, da, dc0, dc1, dc_give, sums, sums_b = refs[16:24]
+    wo, wi, wu, sems = refs[24:]
+    unit = wo.shape[0] // 16
+    copy_o = copies(b_p, wo, place, sems, 0, 1, 4 * unit, unit)
+    copy_i = copies(a_p, wi, place, sems, 32, 4, 0, unit)
+    copy_u = copies(b_p, wu, place, sems, 160, 1, 0, 4 * unit)
+    for copy in copy_u + copy_i + copy_o:
+        copy.start()
+    group = place[5]
+    for copy in copy_u + copy_i:
+        copy.wait()
+    step = 512
+    incoming = dz2[...]
+    for j in range(wu.shape[0] // step):
+        at = slice(step * j, step * (j + 1))
+        grad = low(right_product(df_ref[...], wu[at, :]) * gp_ref[:, at])
+        du[:, at] = grad
+        sums_b[0:1, at] = jnp.sum(grad.astype(F32), 0, keepdims=True)
+        incoming = incoming + right_product(grad, wi[:, at])
+    for copy in copy_o:
+        copy.wait()
+    grad, gain_grad, shift_grad = norm_backward(incoming, n1[...], r1[:, 0:1], vec[3:4, :])
+    grad_out[...] = grad
+    grad_low = low(grad)
+    da[...] = grad_low
+    sums[0:1, :] = gain_grad[None]
+    sums[1:2, :] = shift_grad[None]
+    sums[2:3, :] = jnp.sum(grad_low.astype(F32), 0, keepdims=True)
+    cut = dc0.shape[1]
+    for mask in (1, 3, 0, 2):
+        at = pl.ds(pl.multiple_of((group ^ mask) * cut, 64), cut)
+        part = low(right_product(grad_low, wo[at, :]))
+        if mask % 2:
+            dc_give[mask // 2] = part
+        else:
+            (dc0, dc1)[mask // 2][...] = part
+
+
+def inner_grad_kernel(place, h1b_ref, du, da, c0, c1, c2, c3, give, keep, turned, cs):
+    c, group = place[4], place[5]
+    turned[...] = jnp.transpose(h1b_ref[...])
+    for mask, part in enumerate((c0, c1, c2, c3)):
+        cs[mask] = part[...]
+    unit, cols = give.shape[2] // 5, give.shape[3]
+    blocks = 5
+    wide = (blocks - 1) * cols
+    for half in range(2):
+        side = c ^ 1 ^ half
+        right = du[:, pl.ds(pl.multiple_of(side * wide, 128), wide)]
+        right_low = da[:, pl.ds(pl.multiple_of(side * cols, 128), cols)]
+        for k in range(4):
+            block = block_at(place, k)
+            at = pl.ds(pl.multiple_of(block * (4 * unit), 64), 4 * unit)
+            piece = low(product(turned[at, :], right))
+            tail = low(left_product(cs[block ^ group], right_low))
+            for a in range(4):
+                u = unit_at(place, a)
+                rows = slice(unit * a, unit * (a + 1))
+                for j in range(blocks):
+                    part = piece[rows, cols * j : cols * (j + 1)] if j < blocks - 1 else tail[rows, :]
+                    (give, keep)[half][k, u, unit * j : unit * (j + 1), :] = part
+
+
+def body_fast(
+    tokens,
+    doc_ids,
+    cotangent,
+    query_weight,
+    key_weight,
+    value_weight,
+    output_weight,
+    query_bias,
+    value_bias,
+    output_bias,
+    first_gain,
+    first_shift,
+    inner_weight,
+    inner_bias,
+    outer_weight,
+    outer_bias,
+    second_gain,
+    second_shift,
+):
+    dp, sp = lax.axis_index("dp"), lax.axis_index("sp")
+    y, x, zh, zl, c = dp // 2, dp % 2, sp // 4, (sp // 2) % 2, sp % 2
+    place = jnp.stack([y, x, zh, zl, c, sp % 4]).astype(jnp.int32)
+    width, hidden, rows = tokens.shape[-1], inner_weight.shape[1], tokens.shape[2]
+    cut, shard = width // 4, query_weight.shape[0]
+    unit = 2 * shard
+    wide = 3 * cut + SIDE
+    own, total = 2 * rows, 8 * rows
+    turn = Turns()
+
+    x_rows = rows + DOC_ROWS
+    cols = hidden // 8
+    x_keep, x_give, w_keep, w_give = call(
+        first_kernel,
+        [((x_rows, width), BF16)] * 2 + [((9, shard, cols), BF16)] * 2,
+        [place, tokens[:, 0], doc_ids[:, 0], inner_weight, outer_weight, output_weight],
+        ["hbm"] * 5,
+        scratch=[pltpu.VMEM((2, rows), jnp.int32), pltpu.SemaphoreType.DMA((24,))],
+        name="first",
+    )
+    from_xzh = swap(x_give, BIT_ZH)
+    got = turn(swap(w_give, BIT_C))
+
+    def zl_half(array):
+        half = array.shape[1] // 2
+        return lax.dynamic_slice_in_dim(array, zl * half, half, 1)
+
+    def far_pair(own_half, other_half):
+        turned = pair(other_half[1:], other_half[:1])
+        return join(zl, own_half, turned, 1)
+
+    a_unit = join(c, w_keep[:4], got[:4], 1)
+    b_unit = jnp.concatenate(
+        [
+            join(c, w_keep[4:8].reshape(4 * shard, cols), got[4:8].reshape(4 * shard, cols)),
+            join(c, w_keep[8], got[8]),
+        ]
+    )
+    from_a2 = swap(a_unit[None], BIT_ZL)
+
+    a_pair = pair(a_unit[None], turn(from_a2))
+    from_a4 = swap(zl_half(a_pair), BIT_ZH)
+    from_b2 = swap(tie(b_unit, a_pair)[None], BIT_ZL)
+    smalls = [
+        query_bias, value_bias, output_bias, first_gain, first_shift,
+        outer_bias, second_gain, second_shift,
+    ] + [inner_bias[shard * q : shard * (q + 1)] for q in range(4)]
+    smalls = list(lax.optimization_barrier((*smalls, a_pair))[:-1])
+    row = lax.broadcasted_iota(jnp.int32, (16, 128), 0)
+    packed = jnp.zeros((16, 128), F32)
+    for n, small in enumerate(smalls):
+        wide_small = jnp.pad(small.astype(F32), (0, 128 - shard))
+        packed = jnp.where(row == n, wide_small[None], packed)
+    q_keep, q_give = call(
+        query_kernel,
+        [((2, shard, wide), BF16)] * 2,
+        [place, tie(query_weight, a_pair), key_weight, value_weight, packed],
+        ["hbm"] * 3 + ["vmem"],
+        scratch=[
+            pltpu.VMEM((3, shard, width), BF16),
+            pltpu.VMEM((4, shard, wide), BF16),
+            pltpu.VMEM((128, 128), F32),
+            pltpu.SemaphoreType.DMA((3,)),
+        ],
+        name="query",
+    )
+    from_qc = swap(turn(q_give), BIT_C)
+    b_pair = pair(b_unit[None], turn(from_b2))
+    q_unit = join(c, q_keep, turn(from_qc), 1)
+    from_qzl = swap(q_unit[1], BIT_ZL)
+    mine = jnp.stack([x_keep, turn(from_xzh)])
+    a_half = turn(from_a4)
+    from_a5 = swap(a_half, BIT_ZL)
+    from_b4 = swap(zl_half(tie(b_pair, a_half)), BIT_ZH)
+    q_pair = jnp.stack([q_unit[0], turn(from_qzl)])
+    a_own = pair(a_pair, far_pair(a_half, turn(from_a5)))
+    from_ax = swap(a_own, BIT_X)
+    from_ay = swap(a_own, BIT_Y)
+    from_xzl = swap(tie(mine, a_own), BIT_ZL)
+    b_half = turn(from_b4)
+    from_b5 = swap(b_half, BIT_ZL)
+    from_qzh = swap(tie(q_pair, b_half), BIT_ZH)
+    a_y = turn(from_ay)
+    a_x = turn(from_ax)
+    b_own = pair(b_pair, far_pair(b_half, turn(from_b5)))
+    x_own = pair(mine, turn(from_xzl))
+    from_xc = swap(x_own, BIT_C)
+    q_own = pair(q_pair, turn(from_qzh))
+    from_qy = swap(tie(q_own, a_y), BIT_Y)
+    from_qx = swap(tie(q_own, a_x), BIT_X)
+    x_other = turn(from_xc)
+    from_a0c = swap(tie(a_own, x_other), BIT_C)
+    q_y = turn(from_qy)
+    from_qxy = swap(q_y, BIT_X)
+    from_by = swap(tie(b_own, q_y), BIT_Y)
+    q_x = turn(from_qx)
+    a_c = [turn(from_a0c)]
+    from_a1c = swap(tie(a_x, a_c[0]), BIT_C)
+    a_c.append(turn(from_a1c))
+    q_xy = turn(from_qxy)
+    from_bx = swap(tie(b_own, q_xy), BIT_X)
+    w_attend = [q_own, q_x, q_y, q_xy]
+
+    results = call(
+        attend_kernel,
+        [((2, own, cut), BF16)] * 2
+        + [((total, cut), BF16)] * 3
+        + [((total, cut), F32), ((8, total), F32), ((16, width), F32), ((8, total), F32)],
+        [place, *w_attend, x_own, x_other],
+        scratch=[pltpu.VMEM((width, wide), BF16), pltpu.VMEM((total, 128), F32)],
+        flops=2 * total * width * 3 * cut + 4 * total * total * cut * 4,
+        traffic=8 * total * width,
+        name="attend",
+    )
+    context_keep, context_give, queries, keys, values, context_wide, lse, vec, docs = results
+    context_give = turn(context_give)
+    b_y = turn(from_by)
+    b_x = turn(from_bx)
+    from_axy = swap(tie(a_y, b_x), BIT_X)
+    from_bxy = swap(tie(b_x, b_y), BIT_Y)
+    from_cc = swap(tie(context_give, b_x), BIT_C)
+    from_a2c = swap(tie(a_y, b_x), BIT_C)
+    got = turn(from_cc)
+    from_czl = swap(pair(context_keep[1:], got[1:]), BIT_ZL)
+    context = [context_keep[0], got[0]]
+    a_c.append(turn(from_a2c))
+    from_b0c = swap(tie(b_own, a_c[2]), BIT_C)
+    b_c = [turn(from_b0c)]
+    from_b1c = swap(tie(b_x, b_c[0]), BIT_C)
+    got = turn(from_czl)
+    context += [got[0], got[1]]
+    b_c.append(turn(from_b1c))
+    from_b2c = swap(tie(b_y, b_c[1]), BIT_C)
+    b_inner = jnp.transpose(tie(vec, b_c[1])[8:12].reshape(4, 32, shard), (1, 0, 2)).reshape(1, hidden)
+    b_inner = turn(b_inner)
+    cot_keep = lax.dynamic_index_in_dim(cotangent[:, 0], zh, 0, False)
+    cot_give = turn(lax.dynamic_index_in_dim(cotangent[:, 0], 1 - zh, 0, False))
+    from_cot = swap(cot_give, BIT_ZH)
+    b_c.append(turn(from_b2c))
+    a_xy = turn(from_axy)
+    from_a3c = swap(a_xy, BIT_C)
+    b_xy = turn(from_bxy)
+    from_b3c = swap(b_xy, BIT_C)
+    a_c.append(turn(from_a3c))
+    b_c.append(turn(from_b3c))
+    a_pieces = [a_own, a_x, a_y, a_xy, *a_c]
+    b_pieces = [b_own, b_x, b_y, b_xy, *b_c]
+
+    whole = [
+        pltpu.VMEM((width, width), BF16),
+        pltpu.VMEM((width, hidden), BF16),
+        pltpu.VMEM((hidden, width), BF16),
+        pltpu.SemaphoreType.DMA((192,)),
+    ]
+    results = call(
+        forward_kernel,
+        [
+            ((own, width), BF16), ((own, width), F32), ((own, 128), F32), ((own, width), BF16),
+            ((own, width), F32), ((own, 128), F32), ((own, hidden), BF16), ((own, hidden), F32),
+        ],
+        [place, *context, mine, turn(vec), b_inner, *a_pieces, *b_pieces],
+        ["vmem"] * 7 + ["hbm"] * 16,
+        whole,
+        flops=4 * own * width * hidden * 2,
+        traffic=4 * width * hidden * 2,
+        name="forward",
+    )
+    second_out, second_normed, second_inverse, first_low, normed, inverse, active, slope = results
+    second_normed = turn(second_normed)
+
+    def to_place(kept, other):
+        return join(zh, kept[None], other[None].astype(kept.dtype))[:, None]
+
+    def split(both):
+        half = both.shape[2] // 2
+        return both[:, :, :half], both[:, :, half:]
+
+    def first_hop(both):
+        left, right = split(both)
+        return swap(jnp.stack([left[1], left[3]]), BIT_X), swap(right[2:], BIT_Y)
+
+    def second_hop(both, from_x, from_y):
+        left, right = split(both)
+        return (
+            (add_low(left[0], from_x[0]), add_low(right[0], from_y[0])),
+            swap(add_low(left[2], from_x[1]), BIT_Y),
+            swap(add_low(right[1], from_y[1]), BIT_X),
+        )
+
+    def last_hop(owns, from_y, from_x):
+        return jnp.concatenate([add_low(owns[0], from_y), add_low(owns[1], from_x)], 1)
+
+    def zl_halves(array):
+        half = array.shape[1] // 2
+        one, two = array[:, :half], array[:, half:]
+        return jnp.where(zl == 0, one, two), jnp.where(zl == 0, two, one)
+
+    cot_other = turn(from_cot)
+    b_shape, a_shape = ((4, 4, 4 * unit, cols), BF16), ((4, 4, 5 * unit, cols), BF16)
+    b_give, b_keep, second_grad, outer_grad, sums_a = call(
+        outer_grad_kernel,
+        [b_shape, b_shape, ((own, width), F32), ((own, width), BF16), ((8, width), F32)],
+        [place, cot_keep, cot_other, second_normed, second_inverse, vec, active],
+        name="outer_grad",
+    )
+    b_all = add_low(b_keep, turn(swap(b_give, BIT_C)))
+    from_bx1, from_by1 = first_hop(b_all)
+    outer_grad = tie(outer_grad, b_all)
+    results = call(
+        middle_kernel,
+        [
+            ((own, hidden), BF16), ((own, width), F32), ((own, width), BF16), ((own, cut), BF16),
+            ((own, cut), BF16), ((2, own, cut), BF16), ((8, width), F32), ((8, hidden), F32),
+        ],
+        [place, outer_grad, slope, second_grad, normed, inverse, vec, *a_pieces, *b_pieces],
+        ["vmem"] * 6 + ["hbm"] * 16,
+        whole,
+        flops=4 * own * width * hidden,
+        traffic=6 * width * hidden,
+        name="middle",
+    )
+    inner_grad, first_grad, attended_grad, dc_own, dc_zl, dc_give, sums_c, sums_b = results
+    a_give, a_keep = call(
+        inner_grad_kernel,
+        [a_shape, a_shape],
+        [place, first_low, turn(inner_grad), attended_grad, *context],
+        scratch=[pltpu.VMEM((width, own), BF16), pltpu.VMEM((4, own, cut), BF16)],
+        name="inner_grad",
+    )
+    from_agive = swap(turn(a_give), BIT_C)
+    from_dcc = swap(dc_give, BIT_C)
+    got_x, got_y = turn(from_bx1), turn(from_by1)
+    b_owns, from_by2, from_bx2 = second_hop(b_all, got_x, got_y)
+    got = turn(from_dcc)
+    dc_c = got[0]
+    from_dczl = swap(jnp.stack([dc_zl, got[1]]), BIT_ZL)
+    a_all = add_low(a_keep, turn(from_agive))
+    from_ax1, from_ay1 = first_hop(a_all)
+    b_own = last_hop(b_owns, turn(from_by2), turn(from_bx2))
+    from_bzh = swap(b_own[2:], BIT_ZH)
+    got = turn(from_dczl)
+    dc = [tie(dc_own, b_own), got[0], dc_c, got[1]]
+    grads, sums_d = call(
+        attend_back_kernel,
+        [((total, wide), BF16), ((8, wide), F32)],
+        [place, queries, keys, values, context_wide, lse, *dc, docs],
+        scratch=[
+            pltpu.VMEM((HEAD, total), F32),
+            pltpu.VMEM((8, total), F32),
+            pltpu.VMEM((total, cut), BF16),
+            pltpu.VMEM((total, 128), F32),
+        ],
+        flops=10 * total * total * cut * 4,
+        traffic=8 * total * width,
+        name="attend_back",
+    )
+    grads = turn(grads)
+    from_out = swap(tie(second_out[rows:], grads), BIT_ZH)
+    extra = jnp.concatenate(
+        [
+            sums_c[2:3], sums_c[0:2], sums_a[2:3], sums_a[0:2],
+            jnp.transpose(sums_b[0].reshape(32, 4, shard), (1, 0, 2)).reshape(4, width),
+            jnp.zeros((6, width), F32),
+        ]
+    )
+    results = call(
+        functools.partial(attend_weight_kernel, (3, 2, 1, 0)),
+        [((4, unit, wide), BF16)] * 4 + [((own, width), F32), ((own, width), BF16), ((2, own, width), BF16)],
+        [place, x_own, x_other, grads, *w_attend, sums_d, extra],
+        scratch=[
+            pltpu.VMEM((width, total), BF16),
+            pltpu.VMEM((width, wide), BF16),
+            pltpu.VMEM((width, 128), F32),
+        ],
+        flops=4 * total * width * 3 * cut,
+        traffic=8 * total * width,
+        name="attend_weight",
+    )
+    q_parts, (x_part, x_zl, x_give) = results[:4], results[4:]
+    from_xgive = swap(turn(x_give), BIT_C)
+    b_own = add_low(b_own[:2], turn(from_bzh))
+    from_bzl = swap(b_own[1], BIT_ZL)
+    got_x, got_y = turn(from_ax1), turn(from_ay1)
+    a_owns, from_ay2, from_ax2 = second_hop(a_all, got_x, got_y)
+    got = turn(from_xgive)
+    x_zl = add_low(x_zl, got[1])
+    x_part = x_part + got[0].astype(F32)
+    from_xzl = swap(x_zl, BIT_ZL)
+    outputs = to_place(second_out[:rows], turn(from_out))
+    def core_halves(array, axis):
+        half = array.shape[axis] // 2
+        first_half = lax.slice_in_dim(array, 0, half, axis=axis)
+        last_half = lax.slice_in_dim(array, half, 2 * half, axis=axis)
+        return jnp.where(c == 0, first_half, last_half), jnp.where(c == 0, last_half, first_half)
+
+    b_mine, b_theirs = core_halves(b_own[0].astype(F32) + turn(from_bzl).astype(F32), 0)
+    from_bc = swap(low(b_theirs), BIT_C)
+    a_own = last_hop(a_owns, turn(from_ay2), turn(from_ax2))
+    a_halves = zl_halves(a_own[2:])
+    from_az1 = swap(a_halves[1][::-1], BIT_ZL)
+    from_q1 = swap(tie(q_parts[0], a_own), BIT_X)
+    from_q2 = swap(tie(q_parts[2], a_own), BIT_X)
+    a_far = add_low(a_halves[0], turn(from_az1))
+    from_az2 = swap(a_far, BIT_ZH)
+    x_grad = first_grad + (x_part + turn(from_xzl).astype(F32))
+    outer_owned = join(c, b_mine, turn(from_bc).astype(F32), 1)
+    q_far = add_low(q_parts[1], turn(from_q1))
+    from_q3 = swap(q_far, BIT_Y)
+    q_own = add_low(q_parts[3], turn(from_q2))
+    q_own = add_low(q_own, turn(from_q3))
+    from_qzh = swap(q_own[2:], BIT_ZH)
+    got = turn(from_az2)
+    empty = jnp.zeros_like(got)
+    a_own = add_low(a_own[:2], join(zl, got, empty, 1))
+    from_azl = swap(a_own[1], BIT_ZL)
+    from_xzh = swap(low(tie(x_grad, a_own)[rows:]), BIT_ZH)
+    q_own = add_low(q_own[:2], turn(from_qzh))
+    from_qzl = swap(q_own[1], BIT_ZL)
+    a_last = (a_own[0].astype(F32) + turn(from_azl).astype(F32)).reshape(5, unit, cols)
+    a_mine, a_theirs = core_halves(a_last, 1)
+    from_ac = swap(low(a_theirs), BIT_C)
+    q_two = jnp.stack([q_own[0], turn(from_qzl)])
+    q_mine, q_theirs = core_halves(q_two, 1)
+    from_qc = swap(q_theirs, BIT_C)
+    a_got = turn(from_ac).astype(F32)
+    q_got = turn(from_qc)
+    input_grad = to_place(x_grad[:rows], turn(from_xzh))
+
+    groups = [q_mine[0], q_got[0], q_mine[1], q_got[1]]
+    groups = [part.astype(F32) for part in groups]
+    owned = (groups[0] + groups[1]) + (groups[2] + groups[3])
+    owned = jnp.transpose(owned[:, 3 * cut : 3 * cut + 12])
+
+    def attend_columns(n):
+        parts = [part[:, cut * n : cut * (n + 1)] for part in groups]
+        return join(zl, join(c, parts[0], parts[1], 1), join(c, parts[2], parts[3], 1), 1)
+
+    def inner_columns(array):
+        return jnp.transpose(array[:4], (1, 0, 2)).reshape(shard, 4 * cols)
+
+    inner_owned = join(c, inner_columns(a_mine), inner_columns(a_got), 1)
+    output_owned = join(c, a_mine[4], a_got[4], 1)
+    return (
+        outputs,
+        input_grad,
+        attend_columns(0),
+        attend_columns(1),
+        attend_columns(2),
+        output_owned,
+        owned[0],
+        owned[1],
+        owned[2],
+        owned[3],
+        owned[4],
+        inner_owned,
+        owned[8:12].reshape(-1),
+        outer_owned,
+        owned[5],
+        owned[6],
+        owned[7],
+    )
+
+
 def solution(mesh):
+    fast = mesh.shape["dp"] == 4 and mesh.shape["sp"] == 8
+    body = body_fast if fast else body_general
     in_specs = (
         P(None, "dp", "sp", None),
         P(None, "dp", "sp"),

time: 1370 us -> 308 us (0.22)
  waiting for transfers between devices: 1080 us -> 133 us
  matrix products: 99.7 us -> 0 us
  blocking collectives: 98 us -> 0 us
  Pallas kernels: 0 us -> 66.4 us
  starting transfers between devices: 0.94 us -> 55.9 us
  local copies, waits for them, and re-layouts: 45.4 us -> 21.6 us
    reduce_scatter x5 -> x0, waiting for transfers between devices: 473 us -> none  [the longest x3 387 us: body(): lax.psum_scatter(totals, ('dp', 'sp'), scatter_dimension=0, tiled=True)]
    all_gather x10 -> x0, waiting for transfers between devices: 357 us -> none  [the longest x1 58.5 us: body(): lax.all_gather(shards[1], ('dp', 'sp'), axis=0, tiled=True)]
    unnamed x21 -> x0, waiting for transfers between devices: 245 us -> none
    ppermute x0 -> x62, waiting for transfers between devices: none -> 133 us  [swap(): return lax.ppermute(array, AXES, [(i, i ^ mask) for i in range(32)])]
    dot_general x48 -> x0, matrix products: 99.7 us -> none  [the longest x12 28.2 us: product(): jnp.dot(left_matrix, right_matrix, preferred_element_type=jnp.float32)]
    unnamed x2 -> x0, blocking collectives: 78.7 us -> none
    pallas_call x0 -> x9, Pallas kernels: none -> 66.4 us  [call(): pl.pallas_call(kernel, out_shape=tuple((jax.ShapeDtypeStruct(shape, dtype...]
    ppermute x0 -> x62, starting transfers between devices: none -> 55.9 us  [swap(): return lax.ppermute(array, AXES, [(i, i ^ mask) for i in range(32)])]
  transfers between devices with their start and end apart: 18 -> 62, of which waited for: 18 -> 32; matrix products, arithmetic and copies ran while one was open for 9% -> 11% of each run, Pallas kernels for 0% -> 12%
where the time goes in v1:
time: 308 us; the launch traced here: 305 us
  waiting for transfers between devices  133 us (43%)
  Pallas kernels  66.4 us (22%)
  starting transfers between devices  55.9 us (18%)
  other arithmetic  26.3 us (9%)
  local copies, waits for them, and re-layouts  21.6 us (7%)
    ppermute x62, waiting for transfers between devices, swap(): return lax.ppermute(array, AXES, [(i, i ^ mask) for i in range(32)])  133 us
    pallas_call x9, Pallas kernels, call(): pl.pallas_call(kernel, out_shape=tuple((jax.ShapeDtypeStruct(shape, dtype...  66.4 us
    ppermute x62, starting transfers between devices, swap(): return lax.ppermute(array, AXES, [(i, i ^ mask) for i in range(32)])  55.9 us
    unnamed x92, local copies, waits for them, and re-layouts  9.29 us
    convert_element_type x15, other arithmetic, low(): return array.astype(BF16)  8.75 us
    select_n x17, other arithmetic, join(): jnp.where(bit == 0, jnp.concatenate([own, other], axis), jnp.concatenate(...  7.33 us
  transfers between devices with their start and end apart: 62, of which 32 were waited for; matrix products, arithmetic and copies ran while one was open for 11% of the time, Pallas kernels for 12%

profile of v1, /device:TPU:0, one launch (start us, length us, event | category | flops | bytes accessed | tf_op | source)
XLA Modules:
  0.0 304.8 jit_solution(15553323224403915973)
XLA Ops:
  3.3 3.7 %collective-permute-start.6 = (bf16[144,768]{1,0:T(8,128)(2,1)S(1)}, bf16[144,768]{1,0:T(8,128)(2,1)S(1)}, u32[]{:S(2)}, u32[]{:S(2)}) collective-permute-start(bf16[144,768]{1,0:T(8,128)(2,1)S(1)} %get-tuple-element.193), channel_id=1, source_target_pairs={{0,4},{1,5},{2,6},{3,7},{4,0},{5,1},{6,2},{7,3},{8,12},{9,13},{10,... | collective-permute-start | bytes 663560 | tf_op jit(solution)/shard_map/ppermute | solution.py:356
  9.8 5.6 %collective-permute-done.1 = bf16[1,4,48,384]{3,2,1,0:T(8,128)(2,1)S(1)} collective-permute-done((bf16[1,4,48,384]{3,2,1,0:T(8,128)(2,1)S(1)}, bf16[1,4,48,384]{3,2,1,0:T(8,128)(2,1)S(1)}, u32[]{:S(2)}, u32[]{:S(2)}) %collective-permute-start.1) | collective-permute-done | bytes 147488 | tf_op jit(solution)/shard_map/ppermute | solution.py:356
  15.4 2.5 collective-permute-start.3
  26.2 6.0 %collective-permute-done.5 = bf16[2,2,48,384]{3,2,1,0:T(8,128)(2,1)S(1)} collective-permute-done((bf16[2,2,48,384]{3,2,1,0:T(8,128)(2,1)S(1)}, bf16[2,2,48,384]{3,2,1,0:T(8,128)(2,1)S(1)}, u32[]{:S(2)}, u32[]{:S(2)}) %collective-permute-start.5) | collective-permute-done | bytes 147488 | tf_op jit(solution)/shard_map/ppermute | solution.py:356
  32.3 2.1 collective-permute-start.4
  34.4 4.9 %collective-permute-done.4 = bf16[48,640]{1,0:T(8,128)(2,1)S(1)} collective-permute-done((bf16[48,640]{1,0:T(8,128)(2,1)S(1)}, bf16[48,640]{1,0:T(8,128)(2,1)S(1)}, u32[]{:S(2)}, u32[]{:S(2)}) %collective-permute-start.4) | collective-permute-done | bytes 61472 | tf_op jit(solution)/shard_map/ppermute | solution.py:356
  44.8 10.6 %collective-permute-done.7 = bf16[2,120,384]{2,1,0:T(8,128)(2,1)S(1)} collective-permute-done((bf16[2,120,384]{2,1,0:T(8,128)(2,1)S(1)}, bf16[2,120,384]{2,1,0:T(8,128)(2,1)S(1)}, u32[]{:S(2)}, u32[]{:S(2)}) %collective-permute-start.7) | collective-permute-done | bytes 184352 | tf_op jit(solution)/shard_map/ppermute | solution.py:356
  55.4 2.5 collective-permute-start.11
  57.9 3.5 %collective-permute-done.11 = bf16[2,120,384]{2,1,0:T(8,128)(2,1)S(1)} collective-permute-done((bf16[2,120,384]{2,1,0:T(8,128)(2,1)S(1)}, bf16[2,120,384]{2,1,0:T(8,128)(2,1)S(1)}, u32[]{:S(2)}, u32[]{:S(2)}) %collective-permute-start.11) | collective-permute-done | bytes 184352 | tf_op jit(solution)/shard_map/ppermute | solution.py:356
  61.6 3.0 collective-permute-start.9
  64.6 6.6 %collective-permute-done.9 = bf16[2,48,640]{2,1,0:T(8,128)(2,1)S(1)} collective-permute-done((bf16[2,48,640]{2,1,0:T(8,128)(2,1)S(1)}, bf16[2,48,640]{2,1,0:T(8,128)(2,1)S(1)}, u32[]{:S(2)}, u32[]{:S(2)}) %collective-permute-start.9) | collective-permute-done | bytes 122912 | tf_op jit(solution)/shard_map/ppermute | solution.py:356
  72.4 7.3 %collective-permute-done.15.w2 = bf16[4,48,640]{2,1,0:T(8,128)(2,1)S(1)} collective-permute-done((bf16[4,48,640]{2,1,0:T(8,128)(2,1)S(1)}, bf16[4,48,640]{2,1,0:T(8,128)(2,1)S(1)}, u32[]{:S(2)}, u32[]{:S(2)}) %collective-permute-start.15) | collective-permute-done | bytes 245792 | tf_op jit(solution)/shard_map/ppermute | solution.py:356
  83.3 5.1 %collective-permute-done.17.w3 = bf16[4,48,640]{2,1,0:T(8,128)(2,1)S(1)} collective-permute-done((bf16[4,48,640]{2,1,0:T(8,128)(2,1)S(1)}, bf16[4,48,640]{2,1,0:T(8,128)(2,1)S(1)}, u32[]{:S(2)}, u32[]{:S(2)}) %collective-permute-start.17) | collective-permute-done | bytes 245792 | tf_op jit(solution)/shard_map/ppermute | solution.py:356
  88.9 9.2 %attend.1 = (bf16[2,256,192]{2,1,0:T(8,128)(2,1)S(1)}, bf16[2,256,192]{2,1,0:T(8,128)(2,1)S(1)}, bf16[1024,192]{1,0:T(8,128)(2,1)S(1)}, bf16[1024,192]{1,0:T(8,1...) custom-call(s32[6]{0:T(128)S(1)} %stack.60.place, ...), custom_call_target="tpu_custom_call" | custom-call | flops 1 | bytes 1 | tf_op jit(solution)/shard_map/attend/pallas_call | solution.py:396
  102.1 3.6 %collective-permute-done.20.refs_9_ = bf16[4,240,384]{2,1,0:T(8,128)(2,1)} collective-permute-done((bf16[4,240,384]{2,1,0:T(8,128)(2,1)S(1)}, bf16[4,240,384]{2,1,0:T(8,128)(2,1)}, u32[]{:S(2)}, u32[]{:S(2)}) %collective-permute-start.20) | collective-permute-done | bytes 737312 | tf_op jit(solution)/shard_map/ppermute | solution.py:356
  111.7 8.4 %collective-permute-done.23 = bf16[2,256,192]{2,1,0:T(8,128)(2,1)} collective-permute-done((bf16[2,256,192]{2,1,0:T(8,128)(2,1)S(1)}, bf16[2,256,192]{2,1,0:T(8,128)(2,1)}, u32[]{:S(2)}, u32[]{:S(2)}) %collective-permute-start.23) | collective-permute-done | bytes 196640 | tf_op jit(solution)/shard_map/ppermute | solution.py:356
  127.6 10.2 %collective-permute-done.27.refs_3_ = bf16[4,4,48,384]{3,2,1,0:T(8,128)(2,1)} collective-permute-done((bf16[4,4,48,384]{3,2,1,0:T(8,128)(2,1)}, bf16[4,4,48,384]{3,2,1,0:T(8,128)(2,1)}, u32[]{:S(2)}, u32[]{:S(2)}) %collective-permute-start.27) | collective-permute-done | bytes 589856 | tf_op jit(solution)/shard_map/ppermute | solution.py:356
  144.0 10.5 %forward.1 = (bf16[256,768]{1,0:T(8,128)(2,1)S(1)}, f32[256,768]{1,0:T(8,128)S(1)}, f32[256,128]{1,0:T(8,128)S(1)}, bf16[256,768]{1,0:T(8,128)(2,1)S(1)}, f32[25...) custom-call(s32[6]{0:T(128)S(1)} %stack.60.place, ...), custom_call_target="tpu_custom_call" | custom-call | flops 1 | bytes 1 | tf_op jit(solution)/shard_map/forward/pallas_call | solution.py:396
  154.5 2.5 outer_grad.1
  157.3 4.4 %collective-permute-done.33 = bf16[4,4,192,384]{3,2,1,0:T(8,128)(2,1)S(1)} collective-permute-done((bf16[4,4,192,384]{3,2,1,0:T(8,128)(2,1)S(1)}, bf16[4,4,192,384]{3,2,1,0:T(8,128)(2,1)S(1)}, u32[]{:S(2)}, u32[]{:S(2)}) %collective-permute-start.33) | collective-permute-done | bytes 2359328 | tf_op jit(solution)/shard_map/ppermute | solution.py:356
  162.5 22.2 %middle.1 = (bf16[256,3072]{1,0:T(8,128)(2,1)S(1)}, f32[256,768]{1,0:T(8,128)S(1)}, bf16[256,768]{1,0:T(8,128)(2,1)S(1)}, bf16[256,192]{1,0:T(8,128)(2,1)S(1)}, ...) custom-call(s32[6]{0:T(128)S(1)} %stack.60.place, ...), custom_call_target="tpu_custom_call" | custom-call | flops 1 | bytes 1 | tf_op jit(solution)/shard_map/middle/pallas_call | solution.py:396
  185.6 4.4 %inner_grad.1 = (bf16[4,4,240,384]{3,2,1,0:T(8,128)(2,1)}, bf16[4,4,240,384]{3,2,1,0:T(8,128)(2,1)S(1)}) custom-call(s32[6]{0:T(128)S(1)} %stack.60.place, bf16[256,768]{1,0:T(8,128)(2,1)S(1)} %get-tuple-element.267.h1b_ref, bf16[256,3072]{1,0:T(8,128)(2,1)S(1)} %get-tuple-element.269.du, bf16[256,768]{1,0:T(8,128)(2,1)S(1)} %get-tuple-element.270.da, ...), custom_call_target="tpu_custom_call" | custom-call | flops 1 | bytes 1 | tf_op jit(solution)/shard_map/inner_grad/pallas_call | solution.py:396
  197.1 11.5 %collective-permute-done.34 = bf16[2,4,96,384]{3,2,1,0:T(8,128)(2,1)} collective-permute-done((bf16[2,4,96,384]{3,2,1,0:T(8,128)(2,1)}, bf16[2,4,96,384]{3,2,1,0:T(8,128)(2,1)}, u32[]{:S(2)}, u32[]{:S(2)}) %collective-permute-start.34) | collective-permute-done | bytes 589856 | tf_op jit(solution)/shard_map/ppermute | solution.py:356
  216.3 3.3 %collective-permute-done.35 = bf16[4,96,384]{2,1,0:T(8,128)(2,1)S(1)} collective-permute-done((bf16[4,96,384]{2,1,0:T(8,128)(2,1)S(1)}, bf16[4,96,384]{2,1,0:T(8,128)(2,1)S(1)}, u32[]{:S(2)}, u32[]{:S(2)}) %collective-permute-start.35) | collective-permute-done | bytes 294944 | tf_op jit(solution)/shard_map/ppermute | solution.py:356
  223.5 2.6 add_convert_fusion
  228.7 10.2 %attend_back.1 = (bf16[1024,640]{1,0:T(8,128)(2,1)S(1)}, f32[8,640]{1,0:T(8,128)S(1)}) custom-call(s32[6]{0:T(128)S(1)} %stack.60.place, bf16[1024,192]{1,0:T(8,128)(2,1)S(1)} %copy-done.10, bf16[1024,192]{1,0:T(8,128)(2,1)S(1)} %copy-done.12, bf16[1024,192]{1,0:T(8,128)(2,1)S(1)} %copy-done.14, f32[1024,192]{1,0:T(8,128)S(1)} %copy-done.3, ...), custom_call_target="tpu_custom_call" | custom-call | flops 1 | bytes 1 | tf_op jit(solution)/shard_map/attend_back/pallas_call | solution.py:396
  238.9 4.0 %attend_weight.1 = (bf16[4,48,640]{2,1,0:T(8,128)(2,1)S(1)}, bf16[4,48,640]{2,1,0:T(8,128)(2,1)S(1)}, bf16[4,48,640]{2,1,0:T(8,128)(2,1)S(1)}, bf16[4,48,640]{2,...) custom-call(s32[6]{0:T(128)S(1)} %stack.60.place, ...), custom_call_target="tpu_custom_call" | custom-call | flops 1 | bytes 1 | tf_op jit(solution)/shard_map/attend_weight/pallas_call | solution.py:396
  248.2 7.4 %collective-permute-done.41 = bf16[128,768]{1,0:T(8,128)(2,1)S(1)} collective-permute-done((bf16[128,768]{1,0:T(8,128)(2,1)S(1)}, bf16[128,768]{1,0:T(8,128)(2,1)S(1)}, u32[]{:S(2)}, u32[]{:S(2)}) %collective-permute-start.41) | collective-permute-done | bytes 196640 | tf_op jit(solution)/shard_map/ppermute | solution.py:356
  264.9 8.0 %collective-permute-done.50 = bf16[2,120,384]{2,1,0:T(8,128)(2,1)S(1)} collective-permute-done((bf16[2,120,384]{2,1,0:T(8,128)(2,1)}, bf16[2,120,384]{2,1,0:T(8,128)(2,1)S(1)}, u32[]{:S(2)}, u32[]{:S(2)}) %collective-permute-start.50) | collective-permute-done | bytes 184352 | tf_op jit(solution)/shard_map/ppermute | solution.py:356
  278.3 4.6 %collective-permute-done.54 = bf16[4,48,640]{2,1,0:T(8,128)(2,1)S(1)} collective-permute-done((bf16[4,48,640]{2,1,0:T(8,128)(2,1)S(1)}, bf16[4,48,640]{2,1,0:T(8,128)(2,1)S(1)}, u32[]{:S(2)}, u32[]{:S(2)}) %collective-permute-start.54) | collective-permute-done | bytes 245792 | tf_op jit(solution)/shard_map/ppermute | solution.py:356
  287.8 4.7 %collective-permute-done.57 = bf16[2,48,640]{2,1,0:T(8,128)(2,1)S(1)} collective-permute-done((bf16[2,48,640]{2,1,0:T(8,128)(2,1)S(1)}, bf16[2,48,640]{2,1,0:T(8,128)(2,1)S(1)}, u32[]{:S(2)}, u32[]{:S(2)}) %collective-permute-start.57) | collective-permute-done | bytes 122912 | tf_op jit(solution)/shard_map/ppermute | solution.py:356
  292.6 3.4 %collective-permute-done.59 = bf16[240,384]{1,0:T(8,128)(2,1)S(1)} collective-permute-done((bf16[240,384]{1,0:T(8,128)(2,1)S(1)}, bf16[240,384]{1,0:T(8,128)(2,1)S(1)}, u32[]{:S(2)}, u32[]{:S(2)}) %collective-permute-start.59) | collective-permute-done | bytes 184352 | tf_op jit(solution)/shard_map/ppermute | solution.py:356
  (331 shorter events, 104.2 us)
Async XLA Ops:
  3.3 23.0 %collective-permute-start.6 = (bf16[144,768]{1,0:T(8,128)(2,1)S(1)}, bf16[144,768]{1,0:T(8,128)(2,1)S(1)}, u32[]{:S(2)}, u32[]{:S(2)}) collective-permute-start(bf16[144,768]{1,0:T(8,128)(2,1)S(1)} %get-tuple-element.193), channel_id=1, source_target_pairs={{0,4},{1,5},{2,6},{3,7},{4,0},{5,1},{6,2},{7,3},{8,12},{9,13},{10,... | collective-permute-start | bytes 663560 | tf_op jit(solution)/shard_map/ppermute | solution.py:356
  39.5 18.4 %collective-permute-start.13 = (bf16[4,4,48,384]{3,2,1,0:T(8,128)(2,1)S(1)}, bf16[4,4,48,384]{3,2,1,0:T(8,128)(2,1)}, u32[]{:S(2)}, u32[]{:S(2)}) collective-permute-start(bf16[4,4,48,384]{3,2,1,0:T(8,128)(2,1)S(1)} %pad_maximum_fusion.5.refs_0_), channel_id=1, source_target_pairs={{0,16},{1,17},{2,18},{3,19},{4,20},{5,21},{6,22},{7,23},{8,24},{9,... | collective-permute-start | bytes 1769480 | tf_op jit(solution)/shard_map/ppermute | solution.py:356
  41.1 16.8 %collective-permute-start.12 = (bf16[4,4,48,384]{3,2,1,0:T(8,128)(2,1)S(1)}, bf16[4,4,48,384]{3,2,1,0:T(8,128)(2,1)S(1)}, u32[]{:S(2)}, u32[]{:S(2)}) collective-permute-start(bf16[4,4,48,384]{3,2,1,0:T(8,128)(2,1)S(1)} %pad_maximum_fusion.5.refs_0_), channel_id=1, source_target_pairs={{0,8},{1,9},{2,10},{3,11},{4,12},{5,13},{6,14},{7,15},{8,0},{9,1},... | collective-permute-start | bytes 1769480 | tf_op jit(solution)/shard_map/ppermute | solution.py:356
  42.6 18.8 %collective-permute-start.10 = (bf16[2,144,768]{2,1,0:T(8,128)(2,1)S(1)}, bf16[2,144,768]{2,1,0:T(8,128)(2,1)S(1)}, u32[]{:S(2)}, u32[]{:S(2)}) collective-permute-start(bf16[2,144,768]{2,1,0:T(8,128)(2,1)S(1)} %pad_maximum_fusion.7.x_ref), channel_id=1, source_target_pairs={{0,2},{1,3},{2,0},{3,1},{4,6},{5,7},{6,4},{7,5},{8,10},{9,11},{10,... | collective-permute-start | bytes 1327112 | tf_op jit(solution)/shard_map/ppermute | solution.py:356
  43.0 12.4 %collective-permute-start.7 = (bf16[2,120,384]{2,1,0:T(8,128)(2,1)S(1)}, bf16[2,120,384]{2,1,0:T(8,128)(2,1)S(1)}, u32[]{:S(2)}, u32[]{:S(2)}) collective-permute-start(bf16[2,120,384]{2,1,0:T(8,128)(2,1)S(1)} %constant_dynamic-slice_fusion), channel_id=1, source_target_pairs={{0,4},{1,5},{2,6},{3,7},{4,0},{5,1},{6,2},{7,3},{8,12},{9,13},{10,... | collective-permute-start | bytes 552968 | tf_op jit(solution)/shard_map/ppermute | solution.py:356
  61.5 9.7 %collective-permute-start.16 = (bf16[4,144,768]{2,1,0:T(8,128)(2,1)S(1)}, bf16[4,144,768]{2,1,0:T(8,128)(2,1)S(1)}, u32[]{:S(2)}, u32[]{:S(2)}) collective-permute-start(bf16[4,144,768]{2,1,0:T(8,128)(2,1)S(1)} %pad_maximum_fusion.x_own), channel_id=1, source_target_pairs={{0,1},{1,0},{2,3},{3,2},{4,5},{5,4},{6,7},{7,6},{8,9},{9,8},{10,11... | collective-permute-start | bytes 2654216 | tf_op jit(solution)/shard_map/ppermute | solution.py:356
  61.6 9.6 %collective-permute-start.9 = (bf16[2,48,640]{2,1,0:T(8,128)(2,1)S(1)}, bf16[2,48,640]{2,1,0:T(8,128)(2,1)S(1)}, u32[]{:S(2)}, u32[]{:S(2)}) collective-permute-start(bf16[2,48,640]{2,1,0:T(8,128)(2,1)S(1)} %pad_maximum_fusion.14), channel_id=1, source_target_pairs={{0,4},{1,5},{2,6},{3,7},{4,0},{5,1},{6,2},{7,3},{8,12},{9,13},{10,... | collective-permute-start | bytes 368648 | tf_op jit(solution)/shard_map/ppermute | solution.py:356
  81.7 20.4 %collective-permute-start.21 = (bf16[4,240,384]{2,1,0:T(8,128)(2,1)S(1)}, bf16[4,240,384]{2,1,0:T(8,128)(2,1)}, u32[]{:S(2)}, u32[]{:S(2)}) collective-permute-start(bf16[4,240,384]{2,1,0:T(8,128)(2,1)S(1)} %pad_maximum_fusion.3.refs_8_), channel_id=1, source_target_pairs={{0,16},{1,17},{2,18},{3,19},{4,20},{5,21},{6,22},{7,23},{8,24},{9,... | collective-permute-start | bytes 2211848 | tf_op jit(solution)/shard_map/ppermute | solution.py:356
  88.4 17.3 %collective-permute-start.20 = (bf16[4,240,384]{2,1,0:T(8,128)(2,1)S(1)}, bf16[4,240,384]{2,1,0:T(8,128)(2,1)}, u32[]{:S(2)}, u32[]{:S(2)}) collective-permute-start(bf16[4,240,384]{2,1,0:T(8,128)(2,1)S(1)} %pad_maximum_fusion.3.refs_8_), channel_id=1, source_target_pairs={{0,8},{1,9},{2,10},{3,11},{4,12},{5,13},{6,14},{7,15},{8,0},{9,1},... | collective-permute-start | bytes 2211848 | tf_op jit(solution)/shard_map/ppermute | solution.py:356
  120.4 19.2 %collective-permute-start.26 = (bf16[4,240,384]{2,1,0:T(8,128)(2,1)}, bf16[4,240,384]{2,1,0:T(8,128)(2,1)}, u32[]{:S(2)}, u32[]{:S(2)}) collective-permute-start(bf16[4,240,384]{2,1,0:T(8,128)(2,1)} %collective-permute-done.20.refs_9_), channel_id=1, source_target_pairs={{0,16},{1,17},{2,18},{3,19},{4,20},{5,21},{6,22},{7,23},{8,24},{9,... | collective-permute-start | bytes 2211848 | tf_op jit(solution)/shard_map/ppermute | solution.py:356
  122.0 15.7 %collective-permute-start.27 = (bf16[4,4,48,384]{3,2,1,0:T(8,128)(2,1)}, bf16[4,4,48,384]{3,2,1,0:T(8,128)(2,1)}, u32[]{:S(2)}, u32[]{:S(2)}) collective-permute-start(bf16[4,4,48,384]{3,2,1,0:T(8,128)(2,1)} %collective-permute-done.13.refs_2_), channel_id=1, source_target_pairs={{0,8},{1,9},{2,10},{3,11},{4,12},{5,13},{6,14},{7,15},{8,0},{9,1},... | collective-permute-start | bytes 1769480 | tf_op jit(solution)/shard_map/ppermute | solution.py:356
  140.2 14.3 %collective-permute-start.32 = (bf16[128,768]{1,0:T(8,128)(2,1)}, bf16[128,768]{1,0:T(8,128)(2,1)S(1)}, u32[]{:S(2)}, u32[]{:S(2)}) collective-permute-start(bf16[128,768]{1,0:T(8,128)(2,1)} %get-tuple-element.239), channel_id=1, source_target_pairs={{0,4},{1,5},{2,6},{3,7},{4,0},{5,1},{6,2},{7,3},{8,12},{9,13},{10,... | collective-permute-start | bytes 589832 | tf_op jit(solution)/shard_map/ppermute | solution.py:356
  191.6 24.7 %collective-permute-start.36 = (bf16[4,4,240,384]{3,2,1,0:T(8,128)(2,1)}, bf16[4,4,240,384]{3,2,1,0:T(8,128)(2,1)}, u32[]{:S(2)}, u32[]{:S(2)}) collective-permute-start(bf16[4,4,240,384]{3,2,1,0:T(8,128)(2,1)} %get-tuple-element.272), channel_id=1, source_target_pairs={{0,1},{1,0},{2,3},{3,2},{4,5},{5,4},{6,7},{7,6},{8,9},{9,8},{10,11... | collective-permute-start | bytes 8847368 | tf_op jit(solution)/shard_map/ppermute | solution.py:356
  192.7 15.9 %collective-permute-start.34 = (bf16[2,4,96,384]{3,2,1,0:T(8,128)(2,1)}, bf16[2,4,96,384]{3,2,1,0:T(8,128)(2,1)}, u32[]{:S(2)}, u32[]{:S(2)}) collective-permute-start(bf16[2,4,96,384]{3,2,1,0:T(8,128)(2,1)} %pad_maximum_fusion.6), channel_id=1, source_target_pairs={{0,8},{1,9},{2,10},{3,11},{4,12},{5,13},{6,14},{7,15},{8,0},{9,1},... | collective-permute-start | bytes 1769480 | tf_op jit(solution)/shard_map/ppermute | solution.py:356
  194.2 15.8 %collective-permute-start.38 = (bf16[2,4,96,384]{3,2,1,0:T(8,128)(2,1)}, bf16[2,4,96,384]{3,2,1,0:T(8,128)(2,1)}, u32[]{:S(2)}, u32[]{:S(2)}) collective-permute-start(bf16[2,4,96,384]{3,2,1,0:T(8,128)(2,1)} %slice.473), channel_id=1, source_target_pairs={{0,16},{1,17},{2,18},{3,19},{4,20},{5,21},{6,22},{7,23},{8,24},{9,... | collective-permute-start | bytes 1769480 | tf_op jit(solution)/shard_map/ppermute | solution.py:356
  195.8 14.2 %collective-permute-start.37 = (bf16[2,256,192]{2,1,0:T(8,128)(2,1)}, bf16[2,256,192]{2,1,0:T(8,128)(2,1)S(1)}, u32[]{:S(2)}, u32[]{:S(2)}) collective-permute-start(bf16[2,256,192]{2,1,0:T(8,128)(2,1)} %get-tuple-element.274), channel_id=1, source_target_pairs={{0,1},{1,0},{2,3},{3,2},{4,5},{5,4},{6,7},{7,6},{8,9},{9,8},{10,11... | collective-permute-start | bytes 589832 | tf_op jit(solution)/shard_map/ppermute | solution.py:356
  215.4 11.0 %collective-permute-start.40 = (bf16[2,256,192]{2,1,0:T(8,128)(2,1)S(1)}, bf16[2,256,192]{2,1,0:T(8,128)(2,1)S(1)}, u32[]{:S(2)}, u32[]{:S(2)}) collective-permute-start(bf16[2,256,192]{2,1,0:T(8,128)(2,1)S(1)} %pad_maximum_fusion.11), channel_id=1, source_target_pairs={{0,2},{1,3},{2,0},{3,1},{4,6},{5,7},{6,4},{7,5},{8,10},{9,11},{10,... | collective-permute-start | bytes 589832 | tf_op jit(solution)/shard_map/ppermute | solution.py:356
  222.3 22.5 %collective-permute-start.45 = (bf16[2,192,384]{2,1,0:T(8,128)(2,1)S(1)}, bf16[2,192,384]{2,1,0:T(8,128)(2,1)S(1)}, u32[]{:S(2)}, u32[]{:S(2)}) collective-permute-start(bf16[2,192,384]{2,1,0:T(8,128)(2,1)S(1)} %fusion.16), channel_id=1, source_target_pairs={{0,4},{1,5},{2,6},{3,7},{4,0},{5,1},{6,2},{7,3},{8,12},{9,13},{10,... | collective-permute-start | bytes 884744 | tf_op jit(solution)/shard_map/ppermute | solution.py:356
  226.4 19.4 %collective-permute-start.44 = (bf16[2,4,120,384]{3,2,1,0:T(8,128)(2,1)S(1)}, bf16[2,4,120,384]{3,2,1,0:T(8,128)(2,1)S(1)}, u32[]{:S(2)}, u32[]{:S(2)}) collective-permute-start(bf16[2,4,120,384]{3,2,1,0:T(8,128)(2,1)S(1)} %pad_maximum_fusion.4), channel_id=1, source_target_pairs={{0,8},{1,9},{2,10},{3,11},{4,12},{5,13},{6,14},{7,15},{8,0},{9,1},... | collective-permute-start | bytes 2211848 | tf_op jit(solution)/shard_map/ppermute | solution.py:356
  228.1 17.7 %collective-permute-start.43 = (bf16[2,4,120,384]{3,2,1,0:T(8,128)(2,1)S(1)}, bf16[2,4,120,384]{3,2,1,0:T(8,128)(2,1)S(1)}, u32[]{:S(2)}, u32[]{:S(2)}) collective-permute-start(bf16[2,4,120,384]{3,2,1,0:T(8,128)(2,1)S(1)} %slice.476), channel_id=1, source_target_pairs={{0,16},{1,17},{2,18},{3,19},{4,20},{5,21},{6,22},{7,23},{8,24},{9,... | collective-permute-start | bytes 2211848 | tf_op jit(solution)/shard_map/ppermute | solution.py:356
  243.1 12.5 %collective-permute-start.41 = (bf16[128,768]{1,0:T(8,128)(2,1)S(1)}, bf16[128,768]{1,0:T(8,128)(2,1)S(1)}, u32[]{:S(2)}, u32[]{:S(2)}) collective-permute-start(bf16[128,768]{1,0:T(8,128)(2,1)S(1)} %get-tuple-element.286), channel_id=1, source_target_pairs={{0,4},{1,5},{2,6},{3,7},{4,0},{5,1},{6,2},{7,3},{8,12},{9,13},{10,... | collective-permute-start | bytes 589832 | tf_op jit(solution)/shard_map/ppermute | solution.py:356
  244.9 10.7 %collective-permute-start.49 = (bf16[192,384]{1,0:T(8,128)(2,1)S(1)}, bf16[192,384]{1,0:T(8,128)(2,1)S(1)}, u32[]{:S(2)}, u32[]{:S(2)}) collective-permute-start(bf16[192,384]{1,0:T(8,128)(2,1)S(1)} %slice_bitcast_fusion.7), channel_id=1, source_target_pairs={{0,2},{1,3},{2,0},{3,1},{4,6},{5,7},{6,4},{7,5},{8,10},{9,11},{10,... | collective-permute-start | bytes 442376 | tf_op jit(solution)/shard_map/ppermute | solution.py:356
  246.1 11.9 %collective-permute-start.48 = (bf16[4,120,384]{2,1,0:T(8,128)(2,1)S(1)}, bf16[4,120,384]{2,1,0:T(8,128)(2,1)S(1)}, u32[]{:S(2)}, u32[]{:S(2)}) collective-permute-start(bf16[4,120,384]{2,1,0:T(8,128)(2,1)S(1)} %get-tuple-element.336), channel_id=1, source_target_pairs={{0,16},{1,17},{2,18},{3,19},{4,20},{5,21},{6,22},{7,23},{8,24},{9,... | collective-permute-start | bytes 1105928 | tf_op jit(solution)/shard_map/ppermute | solution.py:356
  247.6 10.3 %collective-permute-start.47 = (bf16[4,120,384]{2,1,0:T(8,128)(2,1)S(1)}, bf16[4,120,384]{2,1,0:T(8,128)(2,1)S(1)}, u32[]{:S(2)}, u32[]{:S(2)}) collective-permute-start(bf16[4,120,384]{2,1,0:T(8,128)(2,1)S(1)} %get-tuple-element.335), channel_id=1, source_target_pairs={{0,8},{1,9},{2,10},{3,11},{4,12},{5,13},{6,14},{7,15},{8,0},{9,1},... | collective-permute-start | bytes 1105928 | tf_op jit(solution)/shard_map/ppermute | solution.py:356
  256.3 16.7 %collective-permute-start.53 = (bf16[96,384]{1,0:T(8,128)(2,1)}, bf16[96,384]{1,0:T(8,128)(2,1)S(1)}, u32[]{:S(2)}, u32[]{:S(2)}) collective-permute-start(bf16[96,384]{1,0:T(8,128)(2,1)} %select_convert_fusion.1), channel_id=1, source_target_pairs={{0,1},{1,0},{2,3},{3,2},{4,5},{5,4},{6,7},{7,6},{8,9},{9,8},{10,11... | collective-permute-start | bytes 221192 | tf_op jit(solution)/shard_map/ppermute | solution.py:356
  257.1 15.8 %collective-permute-start.46 = (bf16[256,768]{1,0:T(8,128)(2,1)}, bf16[256,768]{1,0:T(8,128)(2,1)}, u32[]{:S(2)}, u32[]{:S(2)}) collective-permute-start(bf16[256,768]{1,0:T(8,128)(2,1)} %fusion), channel_id=1, source_target_pairs={{0,2},{1,3},{2,0},{3,1},{4,6},{5,7},{6,4},{7,5},{8,10},{9,11},{10,... | collective-permute-start | bytes 1179656 | tf_op jit(solution)/shard_map/ppermute | solution.py:356
  259.0 13.9 %collective-permute-start.50 = (bf16[2,120,384]{2,1,0:T(8,128)(2,1)}, bf16[2,120,384]{2,1,0:T(8,128)(2,1)S(1)}, u32[]{:S(2)}, u32[]{:S(2)}) collective-permute-start(bf16[2,120,384]{2,1,0:T(8,128)(2,1)} %rev.3), channel_id=1, source_target_pairs={{0,2},{1,3},{2,0},{3,1},{4,6},{5,7},{6,4},{7,5},{8,10},{9,11},{10,... | collective-permute-start | bytes 552968 | tf_op jit(solution)/shard_map/ppermute | solution.py:356
  262.8 15.5 %collective-permute-start.55 = (bf16[4,48,640]{2,1,0:T(8,128)(2,1)S(1)}, bf16[4,48,640]{2,1,0:T(8,128)(2,1)S(1)}, u32[]{:S(2)}, u32[]{:S(2)}) collective-permute-start(bf16[4,48,640]{2,1,0:T(8,128)(2,1)S(1)} %copy-done.28), channel_id=1, source_target_pairs={{0,8},{1,9},{2,10},{3,11},{4,12},{5,13},{6,14},{7,15},{8,0},{9,1},... | collective-permute-start | bytes 737288 | tf_op jit(solution)/shard_map/ppermute | solution.py:356
  263.5 12.4 %collective-permute-start.52 = (bf16[4,48,640]{2,1,0:T(8,128)(2,1)S(1)}, bf16[4,48,640]{2,1,0:T(8,128)(2,1)S(1)}, u32[]{:S(2)}, u32[]{:S(2)}) collective-permute-start(bf16[4,48,640]{2,1,0:T(8,128)(2,1)S(1)} %copy-done.30), channel_id=1, source_target_pairs={{0,8},{1,9},{2,10},{3,11},{4,12},{5,13},{6,14},{7,15},{8,0},{9,1},... | collective-permute-start | bytes 737288 | tf_op jit(solution)/shard_map/ppermute | solution.py:356
  273.0 11.9 %collective-permute-start.51 = (bf16[2,120,384]{2,1,0:T(8,128)(2,1)S(1)}, bf16[2,120,384]{2,1,0:T(8,128)(2,1)S(1)}, u32[]{:S(2)}, u32[]{:S(2)}) collective-permute-start(bf16[2,120,384]{2,1,0:T(8,128)(2,1)S(1)} %add_convert_fusion.15), channel_id=1, source_target_pairs={{0,4},{1,5},{2,6},{3,7},{4,0},{5,1},{6,2},{7,3},{8,12},{9,13},{10,... | collective-permute-start | bytes 552968 | tf_op jit(solution)/shard_map/ppermute | solution.py:356
  285.1 10.9 %collective-permute-start.59 = (bf16[240,384]{1,0:T(8,128)(2,1)S(1)}, bf16[240,384]{1,0:T(8,128)(2,1)S(1)}, u32[]{:S(2)}, u32[]{:S(2)}) collective-permute-start(bf16[240,384]{1,0:T(8,128)(2,1)S(1)} %slice_bitcast_fusion.3), channel_id=1, source_target_pairs={{0,2},{1,3},{2,0},{3,1},{4,6},{5,7},{6,4},{7,5},{8,10},{9,11},{10,... | collective-permute-start | bytes 552968 | tf_op jit(solution)/shard_map/ppermute | solution.py:356
  285.9 14.1 %collective-permute-start.56 = (bf16[128,768]{1,0:T(8,128)(2,1)S(1)}, bf16[128,768]{1,0:T(8,128)(2,1)S(1)}, u32[]{:S(2)}, u32[]{:S(2)}) collective-permute-start(bf16[128,768]{1,0:T(8,128)(2,1)S(1)} %slice.660), channel_id=1, source_target_pairs={{0,4},{1,5},{2,6},{3,7},{4,0},{5,1},{6,2},{7,3},{8,12},{9,13},{10,... | collective-permute-start | bytes 589832 | tf_op jit(solution)/shard_map/ppermute | solution.py:356
  (75 other events, 660.9 us)
